TPU v7x, 256 devices: a whole 4x4x8 slice. The times are simulated.
256 devices in a mesh: gx: 8 (over y, core), gy: 32 (over z, x).
Axes of the slice: x: 4, y: 4, z: 8, core: 2. Of those that a mesh axis runs over, the one named last changes fastest.
Arguments:
- volume: bfloat16 [64, 512, 2048], P('gx', 'gy'), may hold values from -6 to 6
- cotangent: bfloat16 [64, 512, 2048], P('gx', 'gy'), may hold values from -6 to 6
- weight: bfloat16 [3, 3, 3, 32, 32], replicated, may hold values from -0.21875 to 0.21875
- bias: float32 [32], replicated, may hold values from -4 to 4
Outputs:
- data_grad: bfloat16 [64, 512, 2048], P('gx', 'gy')
- filter_grad: float32 [3, 3, 3, 32, 32], replicated
- bias_grad: float32 [32], replicated
All inputs are finite; a program needn't handle non-finite values.
Results may differ from a plain program's by a relative error of at most 0.008.
Values may be sent and summed in bfloat16 or wider, within the bound.
A program may use at most 128 MiB of HBM per device.

v0:
```python
import functools
import math

import jax
import jax.numpy as jnp
from jax import lax
from jax.experimental import pallas as pl
from jax.experimental.pallas import tpu as pltpu
from jax.sharding import PartitionSpec as P

C = 32
MESH = pl.DeviceIdType.MESH
BF = jnp.bfloat16
F32 = jnp.float32
X_CHIPS = 4
Z_CHIPS = 8
NT = (((1,), (1,)), ((), ()))


def halves(low, high, mask):
    return jnp.where(mask, low, high)


def shifted(block, amount, keep):
    return jnp.where(keep, pltpu.roll(block, amount, axis=1), jnp.zeros_like(block))


def kernel(scale, comm, vol, cot, wc, bias, dx, df, db, nv, nc, s, c, gp, t1, t2, dq,
           part, part16, rs, xs, zs, fin, ssem, rsem):
    if comm:
        gx = lax.axis_index("gx")
        gy = lax.axis_index("gy")
        ngx = lax.axis_size("gx")
        ngy = lax.axis_size("gy")
        xi = lax.rem(gy, X_CHIPS)
        zi = lax.div(gy, X_CHIPS)

        def at(ax, ay):
            return {"gx": lax.rem(ax + ngx, ngx), "gy": lax.rem(ay + ngy, ngy)}

        diag = [(dx_, dy_) for dx_ in (-1, 1) for dy_ in (-1, 1)]
        gx_peers = [at(gx + k, gy) for k in range(1, 8)]
        x_peers = [at(gx, zi * X_CHIPS + lax.rem(xi + k, X_CHIPS)) for k in range(1, X_CHIPS)]
        z_peers = [at(gx, lax.rem(zi + k, Z_CHIPS) * X_CHIPS + xi) for k in range(1, Z_CHIPS)]
        peers = gx_peers + x_peers + z_peers + [at(gx, gy - 1), at(gx, gy + 1)]
        peers += [at(gx + a, gy + b) for a, b in diag]
        barrier = pltpu.get_barrier_semaphore()
        for peer in peers:
            pl.semaphore_signal(barrier, inc=1, device_id=peer, device_id_type=MESH)

    lane = lax.broadcasted_iota(jnp.int32, (1, 128), 1)
    low = lane < 64
    z_first = (lane % 64) != 0
    z_last = (lane % 64) != 63
    row = lax.broadcasted_iota(jnp.int32, (256, 256), 0)
    col = lax.broadcasted_iota(jnp.int32, (256, 256), 1)
    perm = jnp.where(col == (row % 16) * 16 + row // 16, 1.0, 0.0).astype(BF)

    def turn(src, dst, first, offset):
        for x in range(0, 8, 2):
            parts = [
                jnp.concatenate([src[x + e, :, g * 128:(g + 1) * 128] for g in range(16)], axis=0)
                for e in range(2)
            ]
            out = jnp.dot(perm, jnp.concatenate(parts, axis=1), preferred_element_type=F32).astype(BF)
            dst[first + x, offset:offset + 256] = out[:, :128]
            dst[first + x + 1, offset:offset + 256] = out[:, 128:]

    turn(vol, nv, 2, 32)
    turn(cot, nc, 1, 16)

    copies = []

    def send(index, src, dst, peer):
        copy = pltpu.make_async_remote_copy(
            src_ref=src, dst_ref=dst, send_sem=ssem.at[index], recv_sem=rsem.at[index],
            device_id=peer, device_id_type=MESH)
        copy.start()
        return copy

    if comm:
        pl.semaphore_wait(barrier, len(peers))
        index = 0
        for buf, w, nx, rows in ((nv, 2, 8, 16), (nc, 1, 8, 16)):
            top = w + nx
            r0, r1, r2, r3 = 0, w * 16, (w + rows) * 16, (2 * w + rows) * 16
            xr = {-1: (slice(w, 2 * w), slice(top, top + w)),
                  0: (slice(w, top), slice(w, top)),
                  1: (slice(top - w, top), slice(0, w))}
            yr = {-1: (slice(r1, 2 * r1), slice(r2, r3)),
                  0: (slice(r1, r2), slice(r1, r2)),
                  1: (slice(r2 - r1, r2), slice(r0, r1))}
            for a in (-1, 0, 1):
                for b in (-1, 0, 1):
                    if a == 0 and b == 0:
                        continue
                    copies.append(send(index, buf.at[xr[a][0], yr[b][0]],
                                       buf.at[xr[a][1], yr[b][1]], at(gx + a, gy + b)))
                    index += 1
    else:
        nv[0:2] = jnp.zeros((2, 320, 128), BF)
        nv[10:12] = jnp.zeros((2, 320, 128), BF)
        nv[:, 0:32] = jnp.zeros((12, 32, 128), BF)
        nv[:, 288:320] = jnp.zeros((12, 32, 128), BF)
        nc[0:1] = jnp.zeros((1, 288, 128), BF)
        nc[9:10] = jnp.zeros((1, 288, 128), BF)
        nc[:, 0:16] = jnp.zeros((10, 16, 128), BF)
        nc[:, 272:288] = jnp.zeros((10, 16, 128), BF)

    for kk in range(9):
        for t, base in ((t1, 0), (t2, 9)):
            w = wc[base + kk].astype(F32)
            for yo in range(6):
                t[yo * 32:(yo + 1) * 32, kk * 256:(kk + 1) * 256] = (
                    w if yo == 0 else pltpu.roll(w, 32 * yo, axis=1)).astype(BF)
    for kz in range(3):
        gp[kz, 576:640] = jnp.zeros((64, 768), BF)

    if comm:
        for copy in copies:
            copy.wait()

        @pl.when(gx == 0)
        def _():
            nv[0:2] = jnp.zeros((2, 320, 128), BF)
            nc[0:1] = jnp.zeros((1, 288, 128), BF)

        @pl.when(gx == ngx - 1)
        def _():
            nv[10:12] = jnp.zeros((2, 320, 128), BF)
            nc[9:10] = jnp.zeros((1, 288, 128), BF)

        @pl.when(gy == 0)
        def _():
            nv[:, 0:32] = jnp.zeros((12, 32, 128), BF)
            nc[:, 0:16] = jnp.zeros((10, 16, 128), BF)

        @pl.when(gy == ngy - 1)
        def _():
            nv[:, 288:320] = jnp.zeros((12, 32, 128), BF)
            nc[:, 272:288] = jnp.zeros((10, 16, 128), BF)

    def paired(buf, j, rows):
        a = buf[j]
        b = buf[j + 4]
        even = jnp.where(low, a, pltpu.roll(b, 64, axis=1))
        odd = jnp.where(low, pltpu.roll(a, 64, axis=1), b)
        both = jnp.concatenate(
            [even.reshape(rows, 1, 16, 128), odd.reshape(rows, 1, 16, 128)], axis=1)
        return both.reshape(rows * 32, 128)

    def fill_s(j, carry):
        block = paired(nv, j, 20)
        lanes = pl.ds(pl.multiple_of(j * 128, 128), 128)
        s[1, :, lanes] = block
        s[0, :, lanes] = shifted(block, 1, z_first)
        s[2, :, lanes] = shifted(block, 127, z_last)
        return carry

    lax.fori_loop(0, 8, fill_s, 0)

    def fill_c(j, carry):
        lanes = pl.ds(pl.multiple_of(j * 128, 128), 128)
        c[:, lanes] = paired(nc, j, 18)
        return carry

    lax.fori_loop(0, 6, fill_c, 0)

    def forward(step, carry):
        b = lax.div(step, 3)
        n = lax.rem(step, 3)
        rows = pl.ds(pl.multiple_of(b * 192, 64), 256)
        out_rows = pl.ds(pl.multiple_of(b * 192, 64), 192)
        out_lanes = pl.ds(pl.multiple_of(n * 256, 128), 256)
        rhs = jnp.concatenate(
            [s[kz, rows, pl.ds(pl.multiple_of(n * 256 + kx * 128, 128), 256)]
             for kx in range(3) for kz in range(3)], axis=0)
        pre = jnp.dot(t1[...], rhs, preferred_element_type=F32) + bias[...]
        sig = 0.5 * jnp.tanh(0.5 * pre) + 0.5
        own = (c[out_rows, out_lanes].astype(F32) * sig * (1.0 + pre * (1.0 - sig))).astype(BF)
        gp[1, out_rows, out_lanes] = own
        for e in range(2):
            piece = own[:, e * 128:(e + 1) * 128]
            lanes = pl.ds(pl.multiple_of(n * 256 + e * 128, 128), 128)
            gp[0, out_rows, lanes] = shifted(piece, 127, z_last)
            gp[2, out_rows, lanes] = shifted(piece, 1, z_first)
        return carry

    lax.fori_loop(0, 9, forward, 0)

    group = lane // 32

    def gathered(wide, tail, rows):
        cells = []
        for q in range(4):
            step = 32 if rows == 96 else 0
            cell = wide[step * q:step * q + rows, :128] + tail[step * q:step * q + rows, :128]
            if q < 2:
                cell = cell + wide[step * (q + 4):step * (q + 4) + rows, 128:]
            cells.append(cell)
        total = jnp.where(group == 0, cells[0], jnp.where(group == 1, cells[1],
                          jnp.where(group == 2, cells[2], cells[3])))
        total = total + pltpu.roll(total, 64, axis=1)
        return total + pltpu.roll(total, 32, axis=1)

    part[...] = jnp.zeros((8, 32, 128), F32)

    def grads(n, count, height):
        return jnp.concatenate([gp[1, 192 * b + 32:192 * b + 32 + height, 128:640]
                                for b in range(n, n + count)], axis=1)

    def filters(kk, carry):
        kx = lax.div(kk, 3)
        kz = lax.rem(kk, 3)
        lanes = pl.ds(pl.multiple_of(kx * 128 + 128, 128), 512)
        left = jnp.concatenate([s[kz, 32:288, lanes], s[kz, 224:480, lanes]], axis=1)
        wide = lax.dot_general(left, grads(0, 2, 256), NT, preferred_element_type=F32)
        tail = lax.dot_general(s[kz, 416:608, lanes], grads(2, 1, 128), NT,
                               preferred_element_type=F32)
        total = gathered(wide, tail, 96)
        for ky in range(3):
            t = kk * 3 + ky
            which = lax.div(t, 4)
            part[which] = jnp.where(group == lax.rem(t, 4), total[ky * 32:(ky + 1) * 32], part[which])
        return carry

    lax.fori_loop(0, 9, filters, 0)
    ones = jnp.ones((16, 1024), BF)
    wide = lax.dot_general(ones, grads(0, 2, 256), NT, preferred_element_type=F32)
    tail = lax.dot_general(ones[:, :512], grads(2, 1, 128), NT, preferred_element_type=F32)
    total = gathered(wide, tail, 16)
    part[6] = jnp.where(group == 3, jnp.concatenate([total, total], axis=0), part[6])

    def backward(b):
        for n in range(2):
            rhs = jnp.concatenate(
                [gp[kz, b * 192:b * 192 + 256, 128 * (2 * n + 2 - kx):128 * (2 * n + 4 - kx)]
                 for kx in range(3) for kz in range(3)], axis=0)
            dq[b * 192:b * 192 + 192, n * 256:n * 256 + 256] = jnp.dot(
                t2[...], rhs, preferred_element_type=F32).astype(BF)

    def emit():
        for j in range(4):
            block = dq[0:512, j * 128:j * 128 + 128].reshape(16, 2, 16, 128)
            even = block[:, 0].reshape(256, 128)
            odd = block[:, 1].reshape(256, 128)
            first = jnp.where(low, even, pltpu.roll(odd, 64, axis=1))
            second = jnp.where(low, pltpu.roll(even, 64, axis=1), odd)
            out = jnp.dot(perm, jnp.concatenate([first, second], axis=1),
                          preferred_element_type=F32).astype(BF)
            for g in range(16):
                dx[j, :, g * 128:(g + 1) * 128] = out[g * 16:(g + 1) * 16, :128]
                dx[j + 4, :, g * 128:(g + 1) * 128] = out[g * 16:(g + 1) * 16, 128:]

    if comm:
        for i in range(8):
            part16[i] = part[i].astype(BF)
        base = 16
        round1 = [send(base + k, part16.at[lax.rem(gx + k + 1, 8)], rs.at[k], gx_peers[k])
                  for k in range(7)]
        backward(0)
        for copy in round1:
            copy.wait()
        mine = part[gx]
        for k in range(7):
            mine = mine + rs[k].astype(F32)
        xs[xi] = mine.astype(BF)
        base += 7
        round2 = [send(base + k, xs.at[xi], xs.at[xi], x_peers[k]) for k in range(X_CHIPS - 1)]
        backward(1)
        for copy in round2:
            copy.wait()
        mine = xs[0].astype(F32)
        for k in range(1, X_CHIPS):
            mine = mine + xs[k].astype(F32)
        zs[zi] = mine.astype(BF)
        base += X_CHIPS - 1
        round3 = [send(base + k, zs.at[zi], zs.at[zi], z_peers[k]) for k in range(Z_CHIPS - 1)]
        backward(2)
        emit()
        for copy in round3:
            copy.wait()
        mine = zs[0].astype(F32)
        for k in range(1, Z_CHIPS):
            mine = mine + zs[k].astype(F32)
        fin[gx] = mine.astype(BF)
        base += Z_CHIPS - 1
        round4 = [send(base + k, fin.at[gx], fin.at[gx], gx_peers[k]) for k in range(7)]
        for copy in round4:
            copy.wait()
    else:
        backward(0)
        backward(1)
        backward(2)
        emit()
        for i in range(8):
            fin[i] = part[i].astype(BF)

    row = lax.broadcasted_iota(jnp.int32, (128, 128), 0)
    col = lax.broadcasted_iota(jnp.int32, (128, 128), 1)
    source = (col // 32) * 32 + (col % 2) * 16 + (col % 32) // 2
    swap = jnp.where(row == source, 1.0, 0.0).astype(BF)
    final = jnp.dot(fin[...].reshape(256, 128), swap, preferred_element_type=F32) * scale
    for t in range(27):
        block = final[(t // 4) * 32:(t // 4) * 32 + 32]
        if t % 4:
            block = pltpu.roll(block, 128 - 32 * (t % 4), axis=1)
        k = (t // 9) * 9 + (t % 3) * 3 + (t // 3) % 3
        df[k, pl.ds(0, 16, stride=2), :] = block[0:16, 0:32]
        df[k, pl.ds(1, 16, stride=2), :] = block[16:32, 0:32]
    db[...] = pltpu.roll(final[192:200], 32, axis=1)[0:1, 0:32]


def shards(comm, cells, volume, cotangent, weight, bias):
    order = jnp.array([2 * (i % 16) + i // 16 for i in range(C)])
    w = weight.reshape(3, 3, 3, 16, 2, 16, 2).transpose(0, 2, 1, 4, 3, 6, 5).reshape(9, 3, C, C)
    fwd = w.transpose(0, 3, 1, 2).reshape(9, C, 3 * C)
    bwd = w[:, ::-1].transpose(0, 2, 1, 3).reshape(9, C, 3 * C)
    wc = jnp.pad(jnp.concatenate([fwd, bwd], axis=0), ((0, 0), (0, 0), (0, 256 - 3 * C)))
    bias_rows = jnp.tile(bias.reshape(16, 2).T.reshape(C), 6).reshape(192, 1)
    vm = pl.BlockSpec(memory_space=pltpu.VMEM)
    dg, df, db = pl.pallas_call(
        functools.partial(kernel, 1.0 / math.sqrt(cells), comm),
        out_shape=(jax.ShapeDtypeStruct(volume.shape, BF),
                   jax.ShapeDtypeStruct((27, C, C), F32),
                   jax.ShapeDtypeStruct((1, C), F32)),
        in_specs=[vm] * 4,
        out_specs=(vm, vm, vm),
        scratch_shapes=[
            pltpu.VMEM((12, 320, 128), BF),
            pltpu.VMEM((10, 288, 128), BF),
            pltpu.VMEM((3, 640, 1024), BF),
            pltpu.VMEM((576, 768), BF),
            pltpu.VMEM((3, 640, 768), BF),
            pltpu.VMEM((192, 2304), BF),
            pltpu.VMEM((192, 2304), BF),
            pltpu.VMEM((576, 512), BF),
            pltpu.VMEM((8, 32, 128), F32),
            pltpu.VMEM((8, 32, 128), BF),
            pltpu.VMEM((7, 32, 128), BF),
            pltpu.VMEM((X_CHIPS, 32, 128), BF),
            pltpu.VMEM((Z_CHIPS, 32, 128), BF),
            pltpu.VMEM((8, 32, 128), BF),
            pltpu.SemaphoreType.DMA((40,)),
            pltpu.SemaphoreType.DMA((40,)),
        ],
        compiler_params=pltpu.CompilerParams(
            collective_id=0 if comm else None, has_side_effects=comm, vmem_limit_bytes=48 << 20),
    )(volume, cotangent, wc, bias_rows)
    return dg, df.reshape(3, 3, 3, C, C), db.reshape(C)


def solution(mesh):
    cells = 8 * mesh.shape["gx"] * 16 * mesh.shape["gy"] * 64
    in_specs = (P("gx", "gy", None), P("gx", "gy", None), P(), P())
    out_specs = (P("gx", "gy", None), P(), P())
    return jax.shard_map(functools.partial(shards, True, cells), mesh=mesh, in_specs=in_specs,
                         out_specs=out_specs, check_vma=False)
```

profile of v0, /device:TPU:1, one launch (start us, length us, event | category | flops | bytes accessed | tf_op | source)
XLA Modules:
  0.0 63.1 jit_solution(10648670606017900463)
XLA Ops:
  0.6 6.0 %reshape.28 = bf16[3,3,3,16,2,16,2]{6,5,4,3,2,1,0:T(8,128)(2,1)} reshape(bf16[3,3,3,32,32]{4,3,2,1,0:T(8,128)(2,1)} %param.6) | data formatting | bytes 110592 | tf_op jit(solution)/shard_map/reshape | solution.py:316
  6.6 0.0 copy-start.2
  6.6 0.0 copy-start
  6.6 0.0 copy-start.1
  6.6 6.6 %copy.10 = bf16[3,3,3,2,16,2,16]{6,5,4,3,2,1,0:T(2,128)(2,1)S(1)} copy(bf16[3,3,3,2,16,2,16]{5,6,3,4,1,2,0:T(8,128)(2,1)} %bitcast.13) | data formatting | bytes 110592 | tf_op jit(solution)/shard_map/transpose | solution.py:316
  13.2 0.2 reshape.29
  13.5 0.2 copy.12
  13.6 0.2 reshape.31
  13.8 0.1 copy.15
  13.9 0.1 fusion.2.wc
  14.0 0.0 copy-done.2
  14.0 0.1 reshape.32
  14.1 0.1 copy.13
  14.2 0.1 tile.7
  14.3 0.1 reshape_tile.4.bias
  14.4 0.0 copy-done
  14.4 0.0 copy-done.1
  14.4 46.6 %shard_map.67 = (bf16[8,16,2048]{2,1,0:T(8,128)(2,1)S(1)}, f32[27,32,32]{2,1,0:T(8,128)S(1)}, f32[1,32]{1,0:T(1,128)S(1)}) custom-call(bf16[8,16,2048]{2,1,0:T(8,128)(2,1)S(1)} %copy-done, bf16[8,16,2048]{2,1,0:T(8,128)(2,1)S(1)} %copy-done.1, bf16[18,32,256]{2,1,0:T(8,128)(2,1)S(1)} %fusion.2.wc, f32[192,1]{1,0:T(8,128)S(1)} %reshape_tile.4.bias), custom_call_target="tpu_custom_call" | custom-call | tf_op jit(solution)/shard_map/pallas_call | solution.py:322
  61.0 0.8 %copy.19 = bf16[8,16,2048]{2,1,0:T(8,128)(2,1)} copy(bf16[8,16,2048]{2,1,0:T(8,128)(2,1)S(1)} %get-tuple-element.12) | data formatting | bytes 1048576
  61.8 0.8 %copy.20 = f32[3,3,3,32,32]{4,3,2,1,0:T(8,128)} copy(f32[3,3,3,32,32]{4,3,2,1,0:T(8,128)S(1)} %bitcast.11) | data formatting | bytes 221184
  62.6 0.5 copy.21
  (2 shorter events, 0.0 us)
Async XLA Ops:
  6.6 7.4 %copy-start.2 = (f32[32]{0:T(128)S(1)}, f32[32]{0:T(128)}, u32[]{:S(2)}) copy-start(f32[32]{0:T(128)} %param.7) | copy-start | bytes 388
  6.6 7.8 %copy-start = (bf16[8,16,2048]{2,1,0:T(8,128)(2,1)S(1)}, bf16[8,16,2048]{2,1,0:T(8,128)(2,1)}, u32[]{:S(2)}) copy-start(bf16[8,16,2048]{2,1,0:T(8,128)(2,1)} %vol.1) | copy-start | bytes 1572868
  6.6 7.8 %copy-start.1 = (bf16[8,16,2048]{2,1,0:T(8,128)(2,1)S(1)}, bf16[8,16,2048]{2,1,0:T(8,128)(2,1)}, u32[]{:S(2)}) copy-start(bf16[8,16,2048]{2,1,0:T(8,128)(2,1)} %cot.1) | copy-start | bytes 1572868
where the time goes:
time: 63.3 us; the launch traced here: 63.1 us
  Pallas kernels  46.6 us (74%)
  local copies, waits for them, and re-layouts  15.7 us (25%)
  between operations  0.72 us (1%)
    pallas_call x1, Pallas kernels, shards(): pl.pallas_call(functools.partial(kernel, 1.0 / math.sqrt(cells), comm), o...  46.6 us
    transpose x1, local copies, waits for them, and re-layouts, shards(): weight.reshape(3, 3, 3, 16, 2, 16, 2).transpose(0, 2, 1, 4, 3, 6, 5)  6.6 us
    reshape x2, local copies, waits for them, and re-layouts, shards(): weight.reshape(3, 3, 3, 16, 2, 16, 2).transpose(0, 2, 1, 4, 3, 6, 5)  6.19 us
    unnamed x9, local copies, waits for them, and re-layouts  2.08 us

commit v1 on v0

v1 whole, which is shorter than its diff:
```python
import functools
import math

import jax
import jax.numpy as jnp
from jax import lax
from jax.experimental import pallas as pl
from jax.experimental.pallas import tpu as pltpu
from jax.sharding import PartitionSpec as P

C = 32
MESH = pl.DeviceIdType.MESH
BF = jnp.bfloat16
F32 = jnp.float32
X_CHIPS = 4
Z_CHIPS = 8
NT = (((1,), (1,)), ((), ()))


def shifted(block, amount, keep):
    return jnp.where(keep, pltpu.roll(block, amount, axis=1), jnp.zeros_like(block))


def natural(index):
    return 2 * (index % 16) + (index % 32) // 16


def one_hot(rows, cols, test):
    row = lax.broadcasted_iota(jnp.int32, (rows, cols), 0)
    col = lax.broadcasted_iota(jnp.int32, (rows, cols), 1)
    return jnp.where(test(row, col), 1.0, 0.0)


def kernel(scale, comm, vol_hbm, cot_hbm, w_hbm, b_hbm, dx, df, db, vol, cot, wbuf, bbuf, nv, nc,
           s, c, gp, t1, t2, tb, dq, part, part16, rs, xs, zs, fin, ssem, rsem, lsem):
    if comm:
        gx = lax.axis_index("gx")
        gy = lax.axis_index("gy")
        ngx = lax.axis_size("gx")
        ngy = lax.axis_size("gy")
        xi = lax.rem(gy, X_CHIPS)
        zi = lax.div(gy, X_CHIPS)

        def at(ax, ay):
            return {"gx": lax.rem(ax + ngx, ngx), "gy": lax.rem(ay + ngy, ngy)}

        around = [(a, b) for a in (-1, 0, 1) for b in (-1, 0, 1) if a or b]
        gx_peers = [at(gx + k, gy) for k in range(1, 8)]
        x_peers = [at(gx, zi * X_CHIPS + lax.rem(xi + k, X_CHIPS)) for k in range(1, X_CHIPS)]
        z_peers = [at(gx, lax.rem(zi + k, Z_CHIPS) * X_CHIPS + xi) for k in range(1, Z_CHIPS)]
        peers = gx_peers + x_peers + z_peers + [at(gx + a, gy + b) for a, b in around if b]
        barrier = pltpu.get_barrier_semaphore()
        for peer in peers:
            pl.semaphore_signal(barrier, inc=1, device_id=peer, device_id_type=MESH)

    loads = [pltpu.make_async_copy(a, b, lsem.at[i]) for i, (a, b) in enumerate(
        ((vol_hbm, vol), (cot_hbm, cot), (w_hbm, wbuf), (b_hbm, bbuf)))]
    for load in loads:
        load.start()

    lane = lax.broadcasted_iota(jnp.int32, (1, 128), 1)
    low = lane < 64
    z_first = (lane % 64) != 0
    z_last = (lane % 64) != 63
    perm = one_hot(256, 256, lambda r, q: q == (r % 16) * 16 + r // 16).astype(BF)

    def turn(src, dst, first, offset):
        for x in range(0, 8, 2):
            parts = [
                jnp.concatenate([src[x + e, :, g * 128:(g + 1) * 128] for g in range(16)], axis=0)
                for e in range(2)
            ]
            out = jnp.dot(perm, jnp.concatenate(parts, axis=1), preferred_element_type=F32).astype(BF)
            dst[first + x, offset:offset + 256] = out[:, :128]
            dst[first + x + 1, offset:offset + 256] = out[:, 128:]

    used = []

    def send(src, dst, peer):
        index = len(used)
        used.append(index)
        copy = pltpu.make_async_remote_copy(
            src_ref=src, dst_ref=dst, send_sem=ssem.at[index], recv_sem=rsem.at[index],
            device_id=peer, device_id_type=MESH)
        copy.start()
        return copy

    def wipe(ref, *shape):
        ref[...] = jnp.zeros(shape, BF)

    loads[0].wait()
    turn(vol, nv, 2, 32)
    if comm:
        pl.semaphore_wait(barrier, len(peers))
        wave1 = [
            send(nv.at[2, 32:288], nv.at[10, 32:288], at(gx - 1, gy)),
            send(nv.at[9, 32:288], nv.at[1, 32:288], at(gx + 1, gy)),
            send(nv.at[2:10, 32:48], nv.at[2:10, 288:304], at(gx, gy - 1)),
            send(nv.at[2:10, 272:288], nv.at[2:10, 16:32], at(gx, gy + 1)),
        ]
        corner_x = {-1: (slice(2, 4), slice(10, 12)), 1: (slice(8, 10), slice(0, 2))}
        corner_y = {-1: (slice(32, 64), slice(288, 320)), 1: (slice(256, 288), slice(0, 32))}
        for a in (-1, 1):
            for b in (-1, 1):
                wave1.append(send(nv.at[corner_x[a][0], corner_y[b][0]],
                                  nv.at[corner_x[a][1], corner_y[b][1]], at(gx + a, gy + b)))
    loads[1].wait()
    turn(cot, nc, 1, 16)
    if comm:
        wave2 = [
            send(nv.at[3, 32:288], nv.at[11, 32:288], at(gx - 1, gy)),
            send(nv.at[8, 32:288], nv.at[0, 32:288], at(gx + 1, gy)),
            send(nv.at[2:10, 48:64], nv.at[2:10, 304:320], at(gx, gy - 1)),
            send(nv.at[2:10, 256:272], nv.at[2:10, 0:16], at(gx, gy + 1)),
        ]
        side_x = {-1: (slice(1, 2), slice(9, 10)), 0: (slice(1, 9), slice(1, 9)),
                  1: (slice(8, 9), slice(0, 1))}
        side_y = {-1: (slice(16, 32), slice(272, 288)), 0: (slice(16, 272), slice(16, 272)),
                  1: (slice(256, 272), slice(0, 16))}
        for a, b in around:
            wave2.append(send(nc.at[side_x[a][0], side_y[b][0]],
                              nc.at[side_x[a][1], side_y[b][1]], at(gx + a, gy + b)))

    def paired(buf, j, r0, r1):
        rows = (r1 - r0) // 16
        a = buf[j, r0:r1]
        b = buf[j + 4, r0:r1]
        even = jnp.where(low, a, pltpu.roll(b, 64, axis=1))
        odd = jnp.where(low, pltpu.roll(a, 64, axis=1), b)
        both = jnp.concatenate(
            [even.reshape(rows, 1, 16, 128), odd.reshape(rows, 1, 16, 128)], axis=1)
        return both.reshape(rows * 32, 128)

    def fill_s(j, y0, y1):
        block = paired(nv, j, y0 * 16, y1 * 16)
        s[1, j, y0 * 32:y1 * 32] = block
        s[0, j, y0 * 32:y1 * 32] = shifted(block, 1, z_first)
        s[2, j, y0 * 32:y1 * 32] = shifted(block, 127, z_last)

    def fill_c(j, y0, y1):
        c[j, y0 * 32:y1 * 32] = paired(nc, j, y0 * 16, y1 * 16)

    @pl.loop(2, 6)
    def _(j):
        fill_s(j, 2, 18)

    @pl.loop(1, 5)
    def _(j):
        fill_c(j, 1, 17)

    def spread(t, kk, base):
        turned = [base] + [pltpu.roll(base, 32 * i, axis=1) for i in (1, 2, 3)]
        zero = jnp.zeros_like(base)
        rows = [(base, zero), (turned[1], zero),
                (jnp.where(lane >= 64, turned[2], zero), jnp.where(lane < 64, turned[2], zero)),
                (jnp.where(lane >= 96, turned[3], zero), jnp.where(lane < 96, turned[3], zero)),
                (zero, base), (zero, turned[1])]
        for yo in range(6):
            for half in range(2):
                t[2 * kk + half, yo * 32:(yo + 1) * 32] = rows[yo][half]

    loads[2].wait()
    loads[3].wait()
    rows4 = one_hot(128, 128, lambda r, q: (r // 32 == q // 32) & (q % 32 == natural(r))).astype(BF)
    lanes1 = one_hot(32, 32, lambda r, q: q == natural(r)).astype(BF)
    stacked = []
    for kk in range(9):
        raw = jnp.concatenate([wbuf[(kk // 3) * 9 + ky * 3 + kk % 3] for ky in range(3)]
                              + [jnp.zeros((32, 32), BF)], axis=0)
        stacked.append(jnp.dot(rows4, raw, preferred_element_type=F32).astype(BF))
        spread(t1, kk, lax.dot_general(lanes1, stacked[kk], NT, preferred_element_type=F32).astype(BF))
    tb[...] = lax.dot_general(
        one_hot(192, 32, lambda r, q: q == natural(r)),
        jnp.broadcast_to(bbuf[...], (128, 32)), NT,
        preferred_element_type=F32, precision=lax.Precision.HIGHEST)

    if comm:
        for copy in wave1:
            copy.wait()

        @pl.when(gx == 0)
        def _():
            wipe(nv.at[1], 320, 128)
            wipe(nv.at[0, 0:32], 32, 128)
            wipe(nv.at[0, 288:320], 32, 128)

        @pl.when(gx == ngx - 1)
        def _():
            wipe(nv.at[10], 320, 128)
            wipe(nv.at[11, 0:32], 32, 128)
            wipe(nv.at[11, 288:320], 32, 128)

        @pl.when(gy == 0)
        def _():
            wipe(nv.at[2:10, 16:32], 8, 16, 128)
            wipe(nv.at[0:2, 0:32], 2, 32, 128)
            wipe(nv.at[10:12, 0:32], 2, 32, 128)

        @pl.when(gy == ngy - 1)
        def _():
            wipe(nv.at[2:10, 288:304], 8, 16, 128)
            wipe(nv.at[0:2, 288:320], 2, 32, 128)
            wipe(nv.at[10:12, 288:320], 2, 32, 128)
    else:
        wipe(nv.at[0:2], 2, 320, 128)
        wipe(nv.at[10:12], 2, 320, 128)
        wipe(nv.at[:, 0:32], 12, 32, 128)
        wipe(nv.at[:, 288:320], 12, 32, 128)
        wipe(nc.at[0], 288, 128)
        wipe(nc.at[9], 288, 128)
        wipe(nc.at[:, 0:16], 10, 16, 128)
        wipe(nc.at[:, 272:288], 10, 16, 128)

    fill_s(1, 1, 19)
    fill_s(6, 1, 19)
    for j in range(2, 6):
        fill_s(j, 1, 2)
        fill_s(j, 18, 19)

    def tiles(buf, kz, cells, r0, r1):
        return jnp.concatenate([buf[kz, cell, r0:r1] for cell in cells], axis=1)

    def filter_rows(t, r0, r1, halves=(0, 1)):
        return jnp.concatenate([t[2 * kk + h, r0:r1] for kk in range(9) for h in halves], axis=1)

    def activate(acc, r0, r1, cells, y):
        for e, cell in enumerate(cells):
            pre = acc[:, e * 128:(e + 1) * 128] + tb[r0:r1]
            sig = 0.5 * jnp.tanh(0.5 * pre) + 0.5
            grad = c[cell, y:y + r1 - r0].astype(F32)
            gp[1, cell, y:y + r1 - r0] = (grad * sig * (1.0 + pre * (1.0 - sig))).astype(BF)

    def forward(r0, r1, y_in, y_out, cells):
        rhs = jnp.concatenate(
            [tiles(s, kz, [cell + kx for cell in cells], y_in * 32, y_in * 32 + 256)
             for kx in range(3) for kz in range(3)], axis=0)
        acc = jnp.dot(filter_rows(t1, r0, r1), rhs, preferred_element_type=F32)
        activate(acc, r0, r1, cells, y_out * 32)

    @pl.loop(0, 2)
    def _(n):
        cells = (2 * n + 1, 2 * n + 2)
        forward(0, 192, 1, 1, cells)
        forward(0, 192, 7, 7, cells)
        forward(64, 192, 11, 13, cells)

    group = lane // 32

    def gathered(wide, tail, rows):
        cells = []
        for q in range(4):
            step = 32 if rows == 96 else 0
            cell = wide[step * q:step * q + rows, :128] + tail[step * q:step * q + rows, :128]
            if q < 2:
                cell = cell + wide[step * (q + 4):step * (q + 4) + rows, 128:]
            cells.append(cell)
        total = jnp.where(group == 0, cells[0], jnp.where(group == 1, cells[1],
                          jnp.where(group == 2, cells[2], cells[3])))
        total = total + pltpu.roll(total, 64, axis=1)
        return total + pltpu.roll(total, 32, axis=1)

    part[...] = jnp.zeros((8, 32, 128), F32)
    own = range(1, 5)

    def grads():
        wide = jnp.concatenate([tiles(gp, 1, own, 32, 288), tiles(gp, 1, own, 224, 480)], axis=1)
        return wide, tiles(gp, 1, own, 416, 544)

    @pl.loop(0, 3)
    def _(kx):
        right, right_tail = grads()
        for kz in range(3):
            cells = [kx + cell for cell in own]
            left = jnp.concatenate([tiles(s, kz, cells, 32, 288), tiles(s, kz, cells, 224, 480)], axis=1)
            wide = lax.dot_general(left, right, NT, preferred_element_type=F32)
            tail = lax.dot_general(tiles(s, kz, cells, 416, 608), right_tail, NT,
                                   preferred_element_type=F32)
            total = gathered(wide, tail, 96)
            for ky in range(3):
                t = kx * 9 + kz * 3 + ky
                which = lax.div(t, 4)
                part[which] = jnp.where(group == lax.rem(t, 4), total[ky * 32:(ky + 1) * 32],
                                        part[which])

    right, right_tail = grads()
    ones = jnp.ones((16, 1024), BF)
    wide = lax.dot_general(ones, right, NT, preferred_element_type=F32)
    tail = lax.dot_general(ones[:, :512], right_tail, NT, preferred_element_type=F32)
    total = gathered(wide, tail, 16)
    part[6] = jnp.where(group == 3, jnp.concatenate([total, total], axis=0), part[6])

    lower = lax.broadcasted_iota(jnp.int32, (32, 128), 0) >= 16

    def split(value, index):
        rounded = value.astype(BF)
        rest = (value - rounded.astype(F32)).astype(BF)
        return jnp.where((index == 6) & (group == 3) & lower, rest, rounded)

    def joined(value, index):
        both = value + jnp.concatenate([value[16:], value[:16]], axis=0)
        return jnp.where((index == 6) & (group == 3), both, value)

    def later_halo():
        base = sum(jnp.dot(jnp.concatenate([stacked_rows(kk, 2 - d) for kk in range(9)], axis=0),
                           one_hot(32, 128, lambda r, q: (q // 32 == d) & (r == natural(q))).astype(BF),
                           preferred_element_type=F32) for d in range(3)).astype(BF)
        for kk in range(9):
            spread(t2, kk, base[kk * 32:(kk + 1) * 32])

        @pl.loop(1, 5)
        def _(j):
            turn_gp(j, 1, 17)

        if comm:
            for copy in wave2:
                copy.wait()

            @pl.when(gx == 0)
            def _():
                wipe(nv.at[0, 32:288], 256, 128)
                wipe(nc.at[0], 288, 128)

            @pl.when(gx == ngx - 1)
            def _():
                wipe(nv.at[11, 32:288], 256, 128)
                wipe(nc.at[9], 288, 128)

            @pl.when(gy == 0)
            def _():
                wipe(nv.at[2:10, 0:16], 8, 16, 128)
                wipe(nc.at[:, 0:16], 10, 16, 128)

            @pl.when(gy == ngy - 1)
            def _():
                wipe(nv.at[2:10, 304:320], 8, 16, 128)
                wipe(nc.at[:, 272:288], 10, 16, 128)

        for j in (0, 7):
            fill_s(j, 0, 20)
        for j in range(1, 7):
            fill_s(j, 0, 1)
            fill_s(j, 19, 20)
        for j in (0, 5):
            fill_c(j, 0, 18)
        for j in own:
            fill_c(j, 0, 1)
            fill_c(j, 17, 18)
        for b in range(3):
            forward(0, 192, 6 * b, 6 * b, (0, 5))
        for cells in ((1, 2), (3, 4)):
            for half, y_in, r0, y_out in ((0, 0, 0, 0), (1, 16, 160, 17)):
                rhs = jnp.concatenate(
                    [tiles(s, kz, [cell + kx for cell in cells], y_in * 32, y_in * 32 + 128)
                     for kx in range(3) for kz in range(3)], axis=0)
                acc = jnp.dot(filter_rows(t1, r0, r0 + 32, (half,)), rhs, preferred_element_type=F32)
                activate(acc, r0, r0 + 32, cells, y_out * 32)
        for j in (0, 5):
            turn_gp(j, 0, 18)
        for j in own:
            turn_gp(j, 0, 1)
            turn_gp(j, 17, 18)

    def stacked_rows(kk, ky):
        return stacked[kk][ky * 32:(ky + 1) * 32]

    def turn_gp(j, y0, y1):
        block = gp[1, j, y0 * 32:y1 * 32]
        gp[0, j, y0 * 32:y1 * 32] = shifted(block, 127, z_last)
        gp[2, j, y0 * 32:y1 * 32] = shifted(block, 1, z_first)

    def backward(b):
        start, r0 = ((0, 0), (6, 0), (10, 64))[b]
        left = filter_rows(t2, r0, 192)
        out = start * 32 + r0
        for n in range(2):
            rhs = jnp.concatenate(
                [tiles(gp, kz, (2 * n + 2 - kx, 2 * n + 3 - kx), start * 32, start * 32 + 256)
                 for kx in range(3) for kz in range(3)], axis=0)
            acc = jnp.dot(left, rhs, preferred_element_type=F32).astype(BF)
            dq[2 * n, out:out + 192 - r0] = acc[:, :128]
            dq[2 * n + 1, out:out + 192 - r0] = acc[:, 128:]

    def emit():
        for j in range(4):
            block = dq[j].reshape(16, 2, 16, 128)
            even = block[:, 0].reshape(256, 128)
            odd = block[:, 1].reshape(256, 128)
            first = jnp.where(low, even, pltpu.roll(odd, 64, axis=1))
            second = jnp.where(low, pltpu.roll(even, 64, axis=1), odd)
            out = jnp.dot(perm, jnp.concatenate([first, second], axis=1),
                          preferred_element_type=F32).astype(BF)
            for g in range(16):
                dx[j, :, g * 128:(g + 1) * 128] = out[g * 16:(g + 1) * 16, :128]
                dx[j + 4, :, g * 128:(g + 1) * 128] = out[g * 16:(g + 1) * 16, 128:]

    def summed(buf, count, index):
        total = buf[0].astype(F32)
        for k in range(1, count):
            total = total + buf[k].astype(F32)
        return joined(total, index)

    for i in range(8):
        part16[i] = split(part[i], i) if i == 6 else part[i].astype(BF)
    if comm:
        round1 = [send(part16.at[lax.rem(gx + k + 1, 8)], rs.at[k], gx_peers[k]) for k in range(7)]
        rs[7] = part16[gx]
        later_halo()
        for copy in round1:
            copy.wait()
        xs[xi] = split(summed(rs, 8, gx), gx)
        round2 = [send(xs.at[xi], xs.at[xi], x_peers[k]) for k in range(X_CHIPS - 1)]
        backward(0)
        backward(1)
        for copy in round2:
            copy.wait()
        zs[zi] = split(summed(xs, X_CHIPS, gx), gx)
        round3 = [send(zs.at[zi], zs.at[zi], z_peers[k]) for k in range(Z_CHIPS - 1)]
        backward(2)
        emit()
        for copy in round3:
            copy.wait()
        fin[gx] = split(summed(zs, Z_CHIPS, gx), gx)
        round4 = [send(fin.at[gx], fin.at[gx], gx_peers[k]) for k in range(7)]
        for copy in round4:
            copy.wait()
    else:
        later_halo()
        backward(0)
        backward(1)
        backward(2)
        emit()
        for i in range(8):
            fin[i] = part16[i]

    swap = one_hot(128, 128, lambda r, q: r == (q // 32) * 32 + (q % 2) * 16 + (q % 32) // 2).astype(BF)
    final = jnp.dot(fin[...].reshape(256, 128), swap, preferred_element_type=F32) * scale
    for t in range(27):
        block = final[(t // 4) * 32:(t // 4) * 32 + 32]
        if t % 4:
            block = pltpu.roll(block, 128 - 32 * (t % 4), axis=1)
        k = (t // 9) * 9 + (t % 3) * 3 + (t // 3) % 3
        df[k, pl.ds(0, 16, stride=2), :] = block[0:16, 0:32]
        df[k, pl.ds(1, 16, stride=2), :] = block[16:32, 0:32]
    db[...] = pltpu.roll(final[192:200] + final[208:216], 32, axis=1)[0:1, 0:32]


def shards(comm, cells, volume, cotangent, weight, bias):
    vm = pl.BlockSpec(memory_space=pltpu.VMEM)
    hbm = pl.BlockSpec(memory_space=pltpu.MemorySpace.HBM)
    dg, df, db = pl.pallas_call(
        functools.partial(kernel, 1.0 / math.sqrt(cells), comm),
        out_shape=(jax.ShapeDtypeStruct(volume.shape, BF),
                   jax.ShapeDtypeStruct((27, C, C), F32),
                   jax.ShapeDtypeStruct((1, C), F32)),
        in_specs=[hbm] * 4,
        out_specs=(vm, vm, vm),
        scratch_shapes=[
            pltpu.VMEM((8, 16, 2048), BF),
            pltpu.VMEM((8, 16, 2048), BF),
            pltpu.VMEM((27, C, C), BF),
            pltpu.VMEM((1, C), F32),
            pltpu.VMEM((12, 320, 128), BF),
            pltpu.VMEM((10, 288, 128), BF),
            pltpu.VMEM((3, 8, 640, 128), BF),
            pltpu.VMEM((6, 576, 128), BF),
            pltpu.VMEM((3, 6, 576, 128), BF),
            pltpu.VMEM((18, 192, 128), BF),
            pltpu.VMEM((18, 192, 128), BF),
            pltpu.VMEM((192, 128), F32),
            pltpu.VMEM((4, 512, 128), BF),
            pltpu.VMEM((8, 32, 128), F32),
            pltpu.VMEM((8, 32, 128), BF),
            pltpu.VMEM((8, 32, 128), BF),
            pltpu.VMEM((X_CHIPS, 32, 128), BF),
            pltpu.VMEM((Z_CHIPS, 32, 128), BF),
            pltpu.VMEM((8, 32, 128), BF),
            pltpu.SemaphoreType.DMA((44,)),
            pltpu.SemaphoreType.DMA((44,)),
            pltpu.SemaphoreType.DMA((4,)),
        ],
        compiler_params=pltpu.CompilerParams(
            collective_id=0 if comm else None, has_side_effects=comm, vmem_limit_bytes=48 << 20),
    )(volume, cotangent, weight.reshape(27, C, C), bias.reshape(1, C))
    return dg, df.reshape(3, 3, 3, C, C), db.reshape(C)


def solution(mesh):
    cells = 8 * mesh.shape["gx"] * 16 * mesh.shape["gy"] * 64
    in_specs = (P("gx", "gy", None), P("gx", "gy", None), P(), P())
    out_specs = (P("gx", "gy", None), P(), P())
    return jax.shard_map(functools.partial(shards, True, cells), mesh=mesh, in_specs=in_specs,
                         out_specs=out_specs, check_vma=False)
```

time: 63.3 us -> 43.7 us (0.69)
  local copies, waits for them, and re-layouts: 15.7 us -> 5.73 us
  Pallas kernels: 46.6 us -> 37.1 us
    pallas_call x1, Pallas kernels: 46.6 us -> 37.1 us  [shards(): pl.pallas_call(functools.partial(kernel, 1.0 / math.sqrt(cells), comm), o...]
    transpose x4 -> x0, local copies, waits for them, and re-layouts: 6.85 us -> none  [the longest x1 6.6 us: shards(): weight.reshape(3, 3, 3, 16, 2, 16, 2).transpose(0, 2, 1, 4, 3, 6, 5)]
    reshape x5 -> x0, local copies, waits for them, and re-layouts: 6.57 us -> none  [the longest x2 6.19 us: shards(): weight.reshape(3, 3, 3, 16, 2, 16, 2).transpose(0, 2, 1, 4, 3, 6, 5)]
    unnamed x9 -> x11, local copies, waits for them, and re-layouts: 2.08 us -> 5.73 us
where the time goes in v1:
time: 43.7 us; the launch traced here: 43.5 us
  Pallas kernels  37.1 us (85%)
  local copies, waits for them, and re-layouts  5.73 us (13%)
  between operations  0.65 us (1%)
    pallas_call x1, Pallas kernels, shards(): pl.pallas_call(functools.partial(kernel, 1.0 / math.sqrt(cells), comm), o...  37.1 us
    unnamed x11, local copies, waits for them, and re-layouts  5.73 us

profile of v1, /device:TPU:1, one launch (start us, length us, event | category | flops | bytes accessed | tf_op | source)
XLA Modules:
  0.0 43.5 jit_solution(1237579572330041557)
XLA Ops:
  0.6 0.0 copy-start.3
  0.6 0.6 %copy-done.3 = f32[32]{0:T(128)S(1)} copy-done((f32[32]{0:T(128)S(1)}, f32[32]{0:T(128)}, u32[]{:S(2)}) %copy-start.3) | copy-done | bytes 152
  1.3 0.0 copy-start
  1.3 1.0 %copy-done = bf16[8,16,2048]{2,1,0:T(8,128)(2,1)S(1)} copy-done((bf16[8,16,2048]{2,1,0:T(8,128)(2,1)S(1)}, bf16[8,16,2048]{2,1,0:T(8,128)(2,1)}, u32[]{:S(2)}) %copy-start) | copy-done | bytes 524312
  2.3 0.0 copy-start.1
  2.3 1.0 %copy-done.1 = bf16[8,16,2048]{2,1,0:T(8,128)(2,1)S(1)} copy-done((bf16[8,16,2048]{2,1,0:T(8,128)(2,1)S(1)}, bf16[8,16,2048]{2,1,0:T(8,128)(2,1)}, u32[]{:S(2)}) %copy-start.1) | copy-done | bytes 524312
  3.4 0.0 copy-start.2
  3.4 0.9 %copy-done.2 = bf16[3,3,3,32,32]{4,3,2,1,0:T(8,128)(2,1)S(1)} copy-done((bf16[3,3,3,32,32]{4,3,2,1,0:T(8,128)(2,1)S(1)}, bf16[3,3,3,32,32]{4,3,2,1,0:T(8,128)(2,1)}, u32[]{:S(2)}) %copy-start.2) | copy-done | bytes 55320
  4.3 37.1 %shard_map.67 = (bf16[8,16,2048]{2,1,0:T(8,128)(2,1)S(1)}, f32[27,32,32]{2,1,0:T(8,128)S(1)}, f32[1,32]{1,0:T(1,128)S(1)}) custom-call(bf16[8,16,2048]{2,1,0:T(8,128)(2,1)S(1)} %copy-done, bf16[8,16,2048]{2,1,0:T(8,128)(2,1)S(1)} %copy-done.1, bf16[27,32,32]{2,1,0:T(8,128)(2,1)S(1)} %bitcast.5, f32[1,32]{1,0:T(1,128)S(1)} %bitcast.6), custom_call_target="tpu_custom_call" | custom-call | tf_op jit(solution)/shard_map/pallas_call | solution.py:450
  41.5 0.8 %copy.10 = bf16[8,16,2048]{2,1,0:T(8,128)(2,1)} copy(bf16[8,16,2048]{2,1,0:T(8,128)(2,1)S(1)} %get-tuple-element.12) | data formatting | bytes 1048576
  42.3 0.8 %copy.11 = f32[3,3,3,32,32]{4,3,2,1,0:T(8,128)} copy(f32[3,3,3,32,32]{4,3,2,1,0:T(8,128)S(1)} %bitcast.4) | data formatting | bytes 221184
  43.0 0.5 %copy.12 = f32[32]{0:T(128)} copy(f32[32]{0:T(128)S(1)} %bitcast.7) | data formatting | bytes 256
Async XLA Ops:
  0.6 0.7 %copy-start.3 = (f32[32]{0:T(128)S(1)}, f32[32]{0:T(128)}, u32[]{:S(2)}) copy-start(f32[32]{0:T(128)} %param.7) | copy-start | bytes 388
  1.3 1.0 %copy-start = (bf16[8,16,2048]{2,1,0:T(8,128)(2,1)S(1)}, bf16[8,16,2048]{2,1,0:T(8,128)(2,1)}, u32[]{:S(2)}) copy-start(bf16[8,16,2048]{2,1,0:T(8,128)(2,1)} %vol_hbm.1) | copy-start | bytes 1572868
  2.3 1.0 %copy-start.1 = (bf16[8,16,2048]{2,1,0:T(8,128)(2,1)S(1)}, bf16[8,16,2048]{2,1,0:T(8,128)(2,1)}, u32[]{:S(2)}) copy-start(bf16[8,16,2048]{2,1,0:T(8,128)(2,1)} %cot_hbm.1) | copy-start | bytes 1572868
  3.4 0.9 %copy-start.2 = (bf16[3,3,3,32,32]{4,3,2,1,0:T(8,128)(2,1)S(1)}, bf16[3,3,3,32,32]{4,3,2,1,0:T(8,128)(2,1)}, u32[]{:S(2)}) copy-start(bf16[3,3,3,32,32]{4,3,2,1,0:T(8,128)(2,1)} %param.6) | copy-start | bytes 165892

commit v2 on v1

--- a/solution.py
+++ b/solution.py
@@ -31,8 +31,8 @@
     return jnp.where(test(row, col), 1.0, 0.0)
 
 
-def kernel(scale, comm, vol_hbm, cot_hbm, w_hbm, b_hbm, dx, df, db, vol, cot, wbuf, bbuf, nv, nc,
-           s, c, gp, t1, t2, tb, dq, part, part16, rs, xs, zs, fin, ssem, rsem, lsem):
+def kernel(comm, vol_hbm, cot_hbm, w_hbm, b_hbm, dx, fin, vol, cot, wbuf, bbuf, nv, nc,
+           s, c, gp, t1, t2, tb, dq, part, part16, rs, xs, zs, ssem, rsem, lsem):
     if comm:
         gx = lax.axis_index("gx")
         gy = lax.axis_index("gy")
@@ -98,28 +98,14 @@
             send(nv.at[2:10, 32:48], nv.at[2:10, 288:304], at(gx, gy - 1)),
             send(nv.at[2:10, 272:288], nv.at[2:10, 16:32], at(gx, gy + 1)),
         ]
-        corner_x = {-1: (slice(2, 4), slice(10, 12)), 1: (slice(8, 10), slice(0, 2))}
-        corner_y = {-1: (slice(32, 64), slice(288, 320)), 1: (slice(256, 288), slice(0, 32))}
+        inner_x = {-1: (2, 10), 1: (9, 1)}
+        inner_y = {-1: (slice(32, 48), slice(288, 304)), 1: (slice(272, 288), slice(16, 32))}
         for a in (-1, 1):
             for b in (-1, 1):
-                wave1.append(send(nv.at[corner_x[a][0], corner_y[b][0]],
-                                  nv.at[corner_x[a][1], corner_y[b][1]], at(gx + a, gy + b)))
+                wave1.append(send(nv.at[inner_x[a][0], inner_y[b][0]],
+                                  nv.at[inner_x[a][1], inner_y[b][1]], at(gx + a, gy + b)))
     loads[1].wait()
     turn(cot, nc, 1, 16)
-    if comm:
-        wave2 = [
-            send(nv.at[3, 32:288], nv.at[11, 32:288], at(gx - 1, gy)),
-            send(nv.at[8, 32:288], nv.at[0, 32:288], at(gx + 1, gy)),
-            send(nv.at[2:10, 48:64], nv.at[2:10, 304:320], at(gx, gy - 1)),
-            send(nv.at[2:10, 256:272], nv.at[2:10, 0:16], at(gx, gy + 1)),
-        ]
-        side_x = {-1: (slice(1, 2), slice(9, 10)), 0: (slice(1, 9), slice(1, 9)),
-                  1: (slice(8, 9), slice(0, 1))}
-        side_y = {-1: (slice(16, 32), slice(272, 288)), 0: (slice(16, 272), slice(16, 272)),
-                  1: (slice(256, 272), slice(0, 16))}
-        for a, b in around:
-            wave2.append(send(nc.at[side_x[a][0], side_y[b][0]],
-                              nc.at[side_x[a][1], side_y[b][1]], at(gx + a, gy + b)))
 
     def paired(buf, j, r0, r1):
         rows = (r1 - r0) // 16
@@ -178,29 +164,45 @@
         for copy in wave1:
             copy.wait()
 
+        wave2 = [
+            send(nv.at[3, 32:288], nv.at[11, 32:288], at(gx - 1, gy)),
+            send(nv.at[8, 32:288], nv.at[0, 32:288], at(gx + 1, gy)),
+            send(nv.at[2:10, 48:64], nv.at[2:10, 304:320], at(gx, gy - 1)),
+            send(nv.at[2:10, 256:272], nv.at[2:10, 0:16], at(gx, gy + 1)),
+        ]
+        outer_x = {-1: (3, 11), 1: (8, 0)}
+        outer_y = {-1: (slice(48, 64), slice(304, 320)), 1: (slice(256, 272), slice(0, 16))}
+        both_y = {-1: (slice(32, 64), slice(288, 320)), 1: (slice(256, 288), slice(0, 32))}
+        for a in (-1, 1):
+            for b in (-1, 1):
+                peer = at(gx + a, gy + b)
+                wave2.append(send(nv.at[outer_x[a][0], both_y[b][0]],
+                                  nv.at[outer_x[a][1], both_y[b][1]], peer))
+                wave2.append(send(nv.at[inner_x[a][0], outer_y[b][0]],
+                                  nv.at[inner_x[a][1], outer_y[b][1]], peer))
+        side_x = {-1: (slice(1, 2), slice(9, 10)), 0: (slice(1, 9), slice(1, 9)),
+                  1: (slice(8, 9), slice(0, 1))}
+        side_y = {-1: (slice(16, 32), slice(272, 288)), 0: (slice(16, 272), slice(16, 272)),
+                  1: (slice(256, 272), slice(0, 16))}
+        for a, b in around:
+            wave2.append(send(nc.at[side_x[a][0], side_y[b][0]],
+                              nc.at[side_x[a][1], side_y[b][1]], at(gx + a, gy + b)))
+
         @pl.when(gx == 0)
         def _():
-            wipe(nv.at[1], 320, 128)
-            wipe(nv.at[0, 0:32], 32, 128)
-            wipe(nv.at[0, 288:320], 32, 128)
+            wipe(nv.at[1, 16:304], 288, 128)
 
         @pl.when(gx == ngx - 1)
         def _():
-            wipe(nv.at[10], 320, 128)
-            wipe(nv.at[11, 0:32], 32, 128)
-            wipe(nv.at[11, 288:320], 32, 128)
+            wipe(nv.at[10, 16:304], 288, 128)
 
         @pl.when(gy == 0)
         def _():
-            wipe(nv.at[2:10, 16:32], 8, 16, 128)
-            wipe(nv.at[0:2, 0:32], 2, 32, 128)
-            wipe(nv.at[10:12, 0:32], 2, 32, 128)
+            wipe(nv.at[1:11, 16:32], 10, 16, 128)
 
         @pl.when(gy == ngy - 1)
         def _():
-            wipe(nv.at[2:10, 288:304], 8, 16, 128)
-            wipe(nv.at[0:2, 288:320], 2, 32, 128)
-            wipe(nv.at[10:12, 288:320], 2, 32, 128)
+            wipe(nv.at[1:11, 288:304], 10, 16, 128)
     else:
         wipe(nv.at[0:2], 2, 320, 128)
         wipe(nv.at[10:12], 2, 320, 128)
@@ -317,22 +319,30 @@
 
             @pl.when(gx == 0)
             def _():
-                wipe(nv.at[0, 32:288], 256, 128)
+                wipe(nv.at[0], 320, 128)
+                wipe(nv.at[1, 0:16], 16, 128)
+                wipe(nv.at[1, 304:320], 16, 128)
                 wipe(nc.at[0], 288, 128)
 
             @pl.when(gx == ngx - 1)
             def _():
-                wipe(nv.at[11, 32:288], 256, 128)
+                wipe(nv.at[11], 320, 128)
+                wipe(nv.at[10, 0:16], 16, 128)
+                wipe(nv.at[10, 304:320], 16, 128)
                 wipe(nc.at[9], 288, 128)
 
             @pl.when(gy == 0)
             def _():
-                wipe(nv.at[2:10, 0:16], 8, 16, 128)
+                wipe(nv.at[:, 0:16], 12, 16, 128)
+                wipe(nv.at[0, 16:32], 16, 128)
+                wipe(nv.at[11, 16:32], 16, 128)
                 wipe(nc.at[:, 0:16], 10, 16, 128)
 
             @pl.when(gy == ngy - 1)
             def _():
-                wipe(nv.at[2:10, 304:320], 8, 16, 128)
+                wipe(nv.at[:, 304:320], 12, 16, 128)
+                wipe(nv.at[0, 288:304], 16, 128)
+                wipe(nv.at[11, 288:304], 16, 128)
                 wipe(nc.at[:, 272:288], 10, 16, 128)
 
         for j in (0, 7):
@@ -432,6 +442,10 @@
         for i in range(8):
             fin[i] = part16[i]
 
+
+def finish(scale, dx, fin, dx_hbm, df_hbm, db_hbm, df, db, sem):
+    out = pltpu.make_async_copy(dx, dx_hbm, sem.at[0])
+    out.start()
     swap = one_hot(128, 128, lambda r, q: r == (q // 32) * 32 + (q % 2) * 16 + (q % 32) // 2).astype(BF)
     final = jnp.dot(fin[...].reshape(256, 128), swap, preferred_element_type=F32) * scale
     for t in range(27):
@@ -442,18 +456,24 @@
         df[k, pl.ds(0, 16, stride=2), :] = block[0:16, 0:32]
         df[k, pl.ds(1, 16, stride=2), :] = block[16:32, 0:32]
     db[...] = pltpu.roll(final[192:200] + final[208:216], 32, axis=1)[0:1, 0:32]
+    others = [pltpu.make_async_copy(df, df_hbm, sem.at[1]), pltpu.make_async_copy(db, db_hbm, sem.at[2])]
+    for copy in others:
+        copy.start()
+    for copy in [out] + others:
+        copy.wait()
 
 
 def shards(comm, cells, volume, cotangent, weight, bias):
     vm = pl.BlockSpec(memory_space=pltpu.VMEM)
     hbm = pl.BlockSpec(memory_space=pltpu.MemorySpace.HBM)
-    dg, df, db = pl.pallas_call(
-        functools.partial(kernel, 1.0 / math.sqrt(cells), comm),
-        out_shape=(jax.ShapeDtypeStruct(volume.shape, BF),
-                   jax.ShapeDtypeStruct((27, C, C), F32),
-                   jax.ShapeDtypeStruct((1, C), F32)),
+    inputs = (volume, cotangent, weight.reshape(27, C, C), bias.reshape(1, C))
+    if comm:
+        inputs = [pltpu.with_memory_space_constraint(a, pltpu.MemorySpace.HBM) for a in inputs]
+    dx, fin = pl.pallas_call(
+        functools.partial(kernel, comm),
+        out_shape=(jax.ShapeDtypeStruct(volume.shape, BF), jax.ShapeDtypeStruct((8, 32, 128), BF)),
         in_specs=[hbm] * 4,
-        out_specs=(vm, vm, vm),
+        out_specs=(vm, vm),
         scratch_shapes=[
             pltpu.VMEM((8, 16, 2048), BF),
             pltpu.VMEM((8, 16, 2048), BF),
@@ -473,14 +493,24 @@
             pltpu.VMEM((8, 32, 128), BF),
             pltpu.VMEM((X_CHIPS, 32, 128), BF),
             pltpu.VMEM((Z_CHIPS, 32, 128), BF),
-            pltpu.VMEM((8, 32, 128), BF),
-            pltpu.SemaphoreType.DMA((44,)),
-            pltpu.SemaphoreType.DMA((44,)),
+            pltpu.SemaphoreType.DMA((52,)),
+            pltpu.SemaphoreType.DMA((52,)),
             pltpu.SemaphoreType.DMA((4,)),
         ],
         compiler_params=pltpu.CompilerParams(
             collective_id=0 if comm else None, has_side_effects=comm, vmem_limit_bytes=48 << 20),
-    )(volume, cotangent, weight.reshape(27, C, C), bias.reshape(1, C))
+    )(*inputs)
+    dg, df, db = pl.pallas_call(
+        functools.partial(finish, 1.0 / math.sqrt(cells)),
+        out_shape=(jax.ShapeDtypeStruct(volume.shape, BF),
+                   jax.ShapeDtypeStruct((27, C, C), F32),
+                   jax.ShapeDtypeStruct((1, C), F32)),
+        in_specs=[vm, vm],
+        out_specs=[pl.BlockSpec(memory_space=pl.ANY)] * 3,
+        scratch_shapes=[pltpu.VMEM((27, C, C), F32), pltpu.VMEM((1, C), F32),
+                        pltpu.SemaphoreType.DMA((3,))],
+        compiler_params=pltpu.CompilerParams(vmem_limit_bytes=4 << 20),
+    )(dx, fin)
     return dg, df.reshape(3, 3, 3, C, C), db.reshape(C)
 
 

time: 43.7 us -> 39 us (0.89)
  local copies, waits for them, and re-layouts: 5.73 us -> 0 us
  Pallas kernels: 37.1 us -> 38.2 us
    unnamed x11 -> x0, local copies, waits for them, and re-layouts: 5.73 us -> none
    pallas_call x1 -> x2, Pallas kernels: 37.1 us -> 38.2 us  [the longest x1 37.1 us: shards(): pl.pallas_call(functools.partial(kernel, comm), out_shape=(jax.ShapeDtype...]
where the time goes in v2:
time: 39 us; the launch traced here: 38.9 us
  Pallas kernels  38.2 us (98%)
  between operations  0.64 us (2%)
    pallas_call x1, Pallas kernels, shards(): pl.pallas_call(functools.partial(kernel, comm), out_shape=(jax.ShapeDtype...  37.1 us
    pallas_call x1, Pallas kernels, shards(): pl.pallas_call(functools.partial(finish, 1.0 / math.sqrt(cells)), out_sha...  1.09 us

profile of v2, /device:TPU:1, one launch (start us, length us, event | category | flops | bytes accessed | tf_op | source)
XLA Modules:
  0.0 38.9 jit_solution(12130149309945489385)
XLA Ops:
  0.6 37.1 %shard_map.67 = (bf16[8,16,2048]{2,1,0:T(8,128)(2,1)S(1)}, bf16[8,32,128]{2,1,0:T(8,128)(2,1)S(1)}) custom-call(bf16[8,16,2048]{2,1,0:T(8,128)(2,1)} %vol_hbm.1, bf16[8,16,2048]{2,1,0:T(8,128)(2,1)} %cot_hbm.1, bf16[27,32,32]{2,1,0:T(8,128)(2,1)} %bitcast.4, f32[1,32]{1,0:T(1,128)} %bitcast.5), custom_call_target="tpu_custom_call" | custom-call | tf_op jit(solution)/shard_map/pallas_call | solution.py:472
  37.8 1.1 %shard_map.68 = (bf16[8,16,2048]{2,1,0:T(8,128)(2,1)}, f32[27,32,32]{2,1,0:T(8,128)}, f32[1,32]{1,0:T(1,128)}) custom-call(bf16[8,16,2048]{2,1,0:T(8,128)(2,1)S(1)} %get-tuple-element.8.dx, bf16[8,32,128]{2,1,0:T(8,128)(2,1)S(1)} %get-tuple-element.9.fin), custom_call_target="tpu_custom_call" | custom-call | tf_op jit(solution)/shard_map/pallas_call | solution.py:503

commit v3 on v2

--- a/solution.py
+++ b/solution.py
@@ -32,7 +32,12 @@
 
 
 def kernel(comm, vol_hbm, cot_hbm, w_hbm, b_hbm, dx, fin, vol, cot, wbuf, bbuf, nv, nc,
-           s, c, gp, t1, t2, tb, dq, part, part16, rs, xs, zs, ssem, rsem, lsem):
+           s, c, gp, t1, t2, tb, dq, part16, rs, xs, zs, ssem, rsem, lsem):
+    loads = [pltpu.make_async_copy(a, b, lsem.at[i]) for i, (a, b) in enumerate(
+        ((vol_hbm, vol), (cot_hbm, cot), (w_hbm, wbuf), (b_hbm, bbuf)))]
+    for load in loads:
+        load.start()
+
     if comm:
         gx = lax.axis_index("gx")
         gy = lax.axis_index("gy")
@@ -48,15 +53,11 @@
         gx_peers = [at(gx + k, gy) for k in range(1, 8)]
         x_peers = [at(gx, zi * X_CHIPS + lax.rem(xi + k, X_CHIPS)) for k in range(1, X_CHIPS)]
         z_peers = [at(gx, lax.rem(zi + k, Z_CHIPS) * X_CHIPS + xi) for k in range(1, Z_CHIPS)]
-        peers = gx_peers + x_peers + z_peers + [at(gx + a, gy + b) for a, b in around if b]
+        peers = z_peers + [at(gx + a, gy + b) for a, b in around if b] + gx_peers + x_peers
         barrier = pltpu.get_barrier_semaphore()
         for peer in peers:
             pl.semaphore_signal(barrier, inc=1, device_id=peer, device_id_type=MESH)
 
-    loads = [pltpu.make_async_copy(a, b, lsem.at[i]) for i, (a, b) in enumerate(
-        ((vol_hbm, vol), (cot_hbm, cot), (w_hbm, wbuf), (b_hbm, bbuf)))]
-    for load in loads:
-        load.start()
 
     lane = lax.broadcasted_iota(jnp.int32, (1, 128), 1)
     low = lane < 64
@@ -239,8 +240,7 @@
         acc = jnp.dot(filter_rows(t1, r0, r1), rhs, preferred_element_type=F32)
         activate(acc, r0, r1, cells, y_out * 32)
 
-    @pl.loop(0, 2)
-    def _(n):
+    for n in range(2):
         cells = (2 * n + 1, 2 * n + 2)
         forward(0, 192, 1, 1, cells)
         forward(0, 192, 7, 7, cells)
@@ -248,49 +248,14 @@
 
     group = lane // 32
 
-    def gathered(wide, tail, rows):
-        cells = []
-        for q in range(4):
-            step = 32 if rows == 96 else 0
-            cell = wide[step * q:step * q + rows, :128] + tail[step * q:step * q + rows, :128]
-            if q < 2:
-                cell = cell + wide[step * (q + 4):step * (q + 4) + rows, 128:]
-            cells.append(cell)
+    def gathered(wide, rows, step):
+        cells = [wide[step * q:step * q + rows, :128] + wide[step * (q + 4):step * (q + 4) + rows, 128:]
+                 for q in range(4)]
         total = jnp.where(group == 0, cells[0], jnp.where(group == 1, cells[1],
                           jnp.where(group == 2, cells[2], cells[3])))
         total = total + pltpu.roll(total, 64, axis=1)
         return total + pltpu.roll(total, 32, axis=1)
 
-    part[...] = jnp.zeros((8, 32, 128), F32)
-    own = range(1, 5)
-
-    def grads():
-        wide = jnp.concatenate([tiles(gp, 1, own, 32, 288), tiles(gp, 1, own, 224, 480)], axis=1)
-        return wide, tiles(gp, 1, own, 416, 544)
-
-    @pl.loop(0, 3)
-    def _(kx):
-        right, right_tail = grads()
-        for kz in range(3):
-            cells = [kx + cell for cell in own]
-            left = jnp.concatenate([tiles(s, kz, cells, 32, 288), tiles(s, kz, cells, 224, 480)], axis=1)
-            wide = lax.dot_general(left, right, NT, preferred_element_type=F32)
-            tail = lax.dot_general(tiles(s, kz, cells, 416, 608), right_tail, NT,
-                                   preferred_element_type=F32)
-            total = gathered(wide, tail, 96)
-            for ky in range(3):
-                t = kx * 9 + kz * 3 + ky
-                which = lax.div(t, 4)
-                part[which] = jnp.where(group == lax.rem(t, 4), total[ky * 32:(ky + 1) * 32],
-                                        part[which])
-
-    right, right_tail = grads()
-    ones = jnp.ones((16, 1024), BF)
-    wide = lax.dot_general(ones, right, NT, preferred_element_type=F32)
-    tail = lax.dot_general(ones[:, :512], right_tail, NT, preferred_element_type=F32)
-    total = gathered(wide, tail, 16)
-    part[6] = jnp.where(group == 3, jnp.concatenate([total, total], axis=0), part[6])
-
     lower = lax.broadcasted_iota(jnp.int32, (32, 128), 0) >= 16
 
     def split(value, index):
@@ -301,6 +266,32 @@
     def joined(value, index):
         both = value + jnp.concatenate([value[16:], value[:16]], axis=0)
         return jnp.where((index == 6) & (group == 3), both, value)
+
+    done = []
+
+    def put(four):
+        value = jnp.where(group == 0, four[0], jnp.where(group == 1, four[1],
+                          jnp.where(group == 2, four[2], four[3])))
+        part16[len(done)] = split(value, len(done)) if len(done) == 6 else value.astype(BF)
+        done.append(0)
+
+    own = range(1, 5)
+    right = jnp.concatenate([tiles(gp, 1, own, 32, 288), tiles(gp, 1, own, 288, 544)], axis=1)
+    blocks = []
+    for kx in range(3):
+        for kz in range(3):
+            cells = [kx + cell for cell in own]
+            left = jnp.concatenate([tiles(s, kz, cells, 32, 352), tiles(s, kz, cells, 288, 608)], axis=1)
+            wide = lax.dot_general(left, right, NT, preferred_element_type=F32)
+            total = gathered(wide, 96, 32)
+            blocks += [total[ky * 32:(ky + 1) * 32] for ky in range(3)]
+            while len(blocks) >= 4:
+                put(blocks[:4])
+                blocks = blocks[4:]
+    wide = lax.dot_general(jnp.ones((16, 1024), BF), right, NT, preferred_element_type=F32)
+    total = gathered(wide, 16, 0)
+    put(blocks + [jnp.concatenate([total, total], axis=0)])
+    part16[7] = jnp.zeros((32, 128), BF)
 
     def later_halo():
         base = sum(jnp.dot(jnp.concatenate([stacked_rows(kk, 2 - d) for kk in range(9)], axis=0),
@@ -409,8 +400,6 @@
             total = total + buf[k].astype(F32)
         return joined(total, index)
 
-    for i in range(8):
-        part16[i] = split(part[i], i) if i == 6 else part[i].astype(BF)
     if comm:
         round1 = [send(part16.at[lax.rem(gx + k + 1, 8)], rs.at[k], gx_peers[k]) for k in range(7)]
         rs[7] = part16[gx]
@@ -488,7 +477,6 @@
             pltpu.VMEM((18, 192, 128), BF),
             pltpu.VMEM((192, 128), F32),
             pltpu.VMEM((4, 512, 128), BF),
-            pltpu.VMEM((8, 32, 128), F32),
             pltpu.VMEM((8, 32, 128), BF),
             pltpu.VMEM((8, 32, 128), BF),
             pltpu.VMEM((X_CHIPS, 32, 128), BF),

time: 39 us -> 36.9 us (0.946)
  Pallas kernels: 38.2 us -> 36.1 us
    pallas_call x1, Pallas kernels: 37.1 us -> 35 us  [shards(): pl.pallas_call(functools.partial(kernel, comm), out_shape=(jax.ShapeDtype...]
where the time goes in v3:
time: 36.9 us; the launch traced here: 36.8 us
  Pallas kernels  36.1 us (98%)
  between operations  0.64 us (2%)
    pallas_call x1, Pallas kernels, shards(): pl.pallas_call(functools.partial(kernel, comm), out_shape=(jax.ShapeDtype...  35 us
    pallas_call x1, Pallas kernels, shards(): pl.pallas_call(functools.partial(finish, 1.0 / math.sqrt(cells)), out_sha...  1.09 us

profile of v3, /device:TPU:1, one launch (start us, length us, event | category | flops | bytes accessed | tf_op | source)
XLA Modules:
  0.0 36.8 jit_solution(15161353143570962532)
XLA Ops:
  0.6 35.0 %shard_map.67 = (bf16[8,16,2048]{2,1,0:T(8,128)(2,1)S(1)}, bf16[8,32,128]{2,1,0:T(8,128)(2,1)S(1)}) custom-call(bf16[8,16,2048]{2,1,0:T(8,128)(2,1)} %vol_hbm.1, bf16[8,16,2048]{2,1,0:T(8,128)(2,1)} %cot_hbm.1, bf16[27,32,32]{2,1,0:T(8,128)(2,1)} %bitcast.4, f32[1,32]{1,0:T(1,128)} %bitcast.5), custom_call_target="tpu_custom_call" | custom-call | tf_op jit(solution)/shard_map/pallas_call | solution.py:461
  35.7 1.1 %shard_map.68 = (bf16[8,16,2048]{2,1,0:T(8,128)(2,1)}, f32[27,32,32]{2,1,0:T(8,128)}, f32[1,32]{1,0:T(1,128)}) custom-call(bf16[8,16,2048]{2,1,0:T(8,128)(2,1)S(1)} %get-tuple-element.8.dx, bf16[8,32,128]{2,1,0:T(8,128)(2,1)S(1)} %get-tuple-element.9.fin), custom_call_target="tpu_custom_call" | custom-call | tf_op jit(solution)/shard_map/pallas_call | solution.py:491

commit v4 on v3

--- a/solution.py
+++ b/solution.py
@@ -32,7 +32,7 @@
 
 
 def kernel(comm, vol_hbm, cot_hbm, w_hbm, b_hbm, dx, fin, vol, cot, wbuf, bbuf, nv, nc,
-           s, c, gp, t1, t2, tb, dq, part16, rs, xs, zs, ssem, rsem, lsem):
+           s, c, gp, t1, t2, tb, dq, part, rs, xs, zs, ssem, rsem, lsem):
     loads = [pltpu.make_async_copy(a, b, lsem.at[i]) for i, (a, b) in enumerate(
         ((vol_hbm, vol), (cot_hbm, cot), (w_hbm, wbuf), (b_hbm, bbuf)))]
     for load in loads:
@@ -256,24 +256,48 @@
         total = total + pltpu.roll(total, 64, axis=1)
         return total + pltpu.roll(total, 32, axis=1)
 
-    lower = lax.broadcasted_iota(jnp.int32, (32, 128), 0) >= 16
-
-    def split(value, index):
+    lower = lax.broadcasted_iota(jnp.int32, (16, 128), 0) >= 8
+
+    def split(chain, value, index):
         rounded = value.astype(BF)
+        if chain == 0:
+            return rounded
         rest = (value - rounded.astype(F32)).astype(BF)
         return jnp.where((index == 6) & (group == 3) & lower, rest, rounded)
 
-    def joined(value, index):
-        both = value + jnp.concatenate([value[16:], value[:16]], axis=0)
-        return jnp.where((index == 6) & (group == 3), both, value)
+    def summed(chain, buf, count, index):
+        total = buf[chain, 0].astype(F32)
+        for k in range(1, count):
+            total = total + buf[chain, k].astype(F32)
+        if chain == 0:
+            return total
+        both = total + jnp.concatenate([total[8:], total[:8]], axis=0)
+        return jnp.where((index == 6) & (group == 3), both, total)
+
+    def scatter(chain):
+        part[chain, 7] = jnp.zeros((16, 128), BF)
+        if not comm:
+            return []
+        copies = [send(part.at[chain, lax.rem(gx + k + 1, 8)], rs.at[chain, k], gx_peers[k])
+                  for k in range(7)]
+        rs[chain, 7] = part[chain, gx]
+        return copies
+
+    def along(buf, chain, slot, peers):
+        return [send(buf.at[chain, slot], buf.at[chain, slot], peer) for peer in peers]
 
     done = []
+    round1 = []
 
     def put(four):
         value = jnp.where(group == 0, four[0], jnp.where(group == 1, four[1],
                           jnp.where(group == 2, four[2], four[3])))
-        part16[len(done)] = split(value, len(done)) if len(done) == 6 else value.astype(BF)
-        done.append(0)
+        for piece in (value[:16], value[16:]):
+            chain, index = divmod(len(done), 7)
+            part[chain, index] = split(chain, piece, index) if index == 6 else piece.astype(BF)
+            done.append(0)
+            if index == 6:
+                round1.append(scatter(chain))
 
     own = range(1, 5)
     right = jnp.concatenate([tiles(gp, 1, own, 32, 288), tiles(gp, 1, own, 288, 544)], axis=1)
@@ -291,7 +315,6 @@
     wide = lax.dot_general(jnp.ones((16, 1024), BF), right, NT, preferred_element_type=F32)
     total = gathered(wide, 16, 0)
     put(blocks + [jnp.concatenate([total, total], axis=0)])
-    part16[7] = jnp.zeros((32, 128), BF)
 
     def later_halo():
         base = sum(jnp.dot(jnp.concatenate([stacked_rows(kk, 2 - d) for kk in range(9)], axis=0),
@@ -394,49 +417,54 @@
                 dx[j, :, g * 128:(g + 1) * 128] = out[g * 16:(g + 1) * 16, :128]
                 dx[j + 4, :, g * 128:(g + 1) * 128] = out[g * 16:(g + 1) * 16, 128:]
 
-    def summed(buf, count, index):
-        total = buf[0].astype(F32)
-        for k in range(1, count):
-            total = total + buf[k].astype(F32)
-        return joined(total, index)
-
+    later_halo()
     if comm:
-        round1 = [send(part16.at[lax.rem(gx + k + 1, 8)], rs.at[k], gx_peers[k]) for k in range(7)]
-        rs[7] = part16[gx]
-        later_halo()
-        for copy in round1:
-            copy.wait()
-        xs[xi] = split(summed(rs, 8, gx), gx)
-        round2 = [send(xs.at[xi], xs.at[xi], x_peers[k]) for k in range(X_CHIPS - 1)]
+        for copy in round1[0]:
+            copy.wait()
+        xs[0, xi] = split(0, summed(0, rs, 8, gx), gx)
+        round2a = along(xs, 0, xi, x_peers)
+        for copy in round1[1]:
+            copy.wait()
+        zs[1, zi] = split(1, summed(1, rs, 8, gx), gx)
+        round2b = along(zs, 1, zi, z_peers)
         backward(0)
+        for copy in round2a:
+            copy.wait()
+        zs[0, zi] = split(0, summed(0, xs, X_CHIPS, gx), gx)
+        round3a = along(zs, 0, zi, z_peers)
         backward(1)
-        for copy in round2:
-            copy.wait()
-        zs[zi] = split(summed(xs, X_CHIPS, gx), gx)
-        round3 = [send(zs.at[zi], zs.at[zi], z_peers[k]) for k in range(Z_CHIPS - 1)]
         backward(2)
         emit()
-        for copy in round3:
-            copy.wait()
-        fin[gx] = split(summed(zs, Z_CHIPS, gx), gx)
-        round4 = [send(fin.at[gx], fin.at[gx], gx_peers[k]) for k in range(7)]
+        for copy in round2b:
+            copy.wait()
+        xs[1, xi] = split(1, summed(1, zs, Z_CHIPS, gx), gx)
+        round3b = along(xs, 1, xi, x_peers)
+        for copy in round3a:
+            copy.wait()
+        fin[0, gx] = split(0, summed(0, zs, Z_CHIPS, gx), gx)
+        round4 = along(fin, 0, gx, gx_peers)
+        for copy in round3b:
+            copy.wait()
+        fin[1, gx] = split(1, summed(1, xs, X_CHIPS, gx), gx)
+        round4 += along(fin, 1, gx, gx_peers)
         for copy in round4:
             copy.wait()
     else:
-        later_halo()
         backward(0)
         backward(1)
         backward(2)
         emit()
         for i in range(8):
-            fin[i] = part16[i]
+            fin[0, i] = part[0, i]
+            fin[1, i] = part[1, i]
 
 
 def finish(scale, dx, fin, dx_hbm, df_hbm, db_hbm, df, db, sem):
     out = pltpu.make_async_copy(dx, dx_hbm, sem.at[0])
     out.start()
     swap = one_hot(128, 128, lambda r, q: r == (q // 32) * 32 + (q % 2) * 16 + (q % 32) // 2).astype(BF)
-    final = jnp.dot(fin[...].reshape(256, 128), swap, preferred_element_type=F32) * scale
+    rows = jnp.concatenate([fin[chain, i] for chain in range(2) for i in range(7)], axis=0)
+    final = jnp.dot(rows, swap, preferred_element_type=F32) * scale
     for t in range(27):
         block = final[(t // 4) * 32:(t // 4) * 32 + 32]
         if t % 4:
@@ -444,7 +472,7 @@
         k = (t // 9) * 9 + (t % 3) * 3 + (t // 3) % 3
         df[k, pl.ds(0, 16, stride=2), :] = block[0:16, 0:32]
         df[k, pl.ds(1, 16, stride=2), :] = block[16:32, 0:32]
-    db[...] = pltpu.roll(final[192:200] + final[208:216], 32, axis=1)[0:1, 0:32]
+    db[...] = pltpu.roll(final[208:216] + final[216:224], 32, axis=1)[0:1, 0:32]
     others = [pltpu.make_async_copy(df, df_hbm, sem.at[1]), pltpu.make_async_copy(db, db_hbm, sem.at[2])]
     for copy in others:
         copy.start()
@@ -460,7 +488,7 @@
         inputs = [pltpu.with_memory_space_constraint(a, pltpu.MemorySpace.HBM) for a in inputs]
     dx, fin = pl.pallas_call(
         functools.partial(kernel, comm),
-        out_shape=(jax.ShapeDtypeStruct(volume.shape, BF), jax.ShapeDtypeStruct((8, 32, 128), BF)),
+        out_shape=(jax.ShapeDtypeStruct(volume.shape, BF), jax.ShapeDtypeStruct((2, 8, 16, 128), BF)),
         in_specs=[hbm] * 4,
         out_specs=(vm, vm),
         scratch_shapes=[
@@ -477,12 +505,12 @@
             pltpu.VMEM((18, 192, 128), BF),
             pltpu.VMEM((192, 128), F32),
             pltpu.VMEM((4, 512, 128), BF),
-            pltpu.VMEM((8, 32, 128), BF),
-            pltpu.VMEM((8, 32, 128), BF),
-            pltpu.VMEM((X_CHIPS, 32, 128), BF),
-            pltpu.VMEM((Z_CHIPS, 32, 128), BF),
-            pltpu.SemaphoreType.DMA((52,)),
-            pltpu.SemaphoreType.DMA((52,)),
+            pltpu.VMEM((2, 8, 16, 128), BF),
+            pltpu.VMEM((2, 8, 16, 128), BF),
+            pltpu.VMEM((2, X_CHIPS, 16, 128), BF),
+            pltpu.VMEM((2, Z_CHIPS, 16, 128), BF),
+            pltpu.SemaphoreType.DMA((76,)),
+            pltpu.SemaphoreType.DMA((76,)),
             pltpu.SemaphoreType.DMA((4,)),
         ],
         compiler_params=pltpu.CompilerParams(

time: 36.9 us -> 38.6 us (1.046)
  Pallas kernels: 36.1 us -> 37.8 us
    pallas_call x1, Pallas kernels: 35 us -> 36.7 us  [shards(): pl.pallas_call(functools.partial(kernel, comm), out_shape=(jax.ShapeDtype...]
where the time goes in v4:
time: 38.6 us; the launch traced here: 38.5 us
  Pallas kernels  37.8 us (98%)
  between operations  0.64 us (2%)
    pallas_call x1, Pallas kernels, shards(): pl.pallas_call(functools.partial(kernel, comm), out_shape=(jax.ShapeDtype...  36.7 us
    pallas_call x1, Pallas kernels, shards(): pl.pallas_call(functools.partial(finish, 1.0 / math.sqrt(cells)), out_sha...  1.09 us

profile of v4, /device:TPU:1, one launch (start us, length us, event | category | flops | bytes accessed | tf_op | source)
XLA Modules:
  0.0 38.5 jit_solution(15318180853244338432)
XLA Ops:
  0.6 36.7 %shard_map.67 = (bf16[8,16,2048]{2,1,0:T(8,128)(2,1)S(1)}, bf16[2,8,16,128]{3,2,1,0:T(8,128)(2,1)S(1)}) custom-call(bf16[8,16,2048]{2,1,0:T(8,128)(2,1)} %vol_hbm.1, bf16[8,16,2048]{2,1,0:T(8,128)(2,1)} %cot_hbm.1, bf16[27,32,32]{2,1,0:T(8,128)(2,1)} %bitcast.4, f32[1,32]{1,0:T(1,128)} %bitcast.5), custom_call_target="tpu_custom_call" | custom-call | tf_op jit(solution)/shard_map/pallas_call | solution.py:489
  37.4 1.1 %shard_map.68 = (bf16[8,16,2048]{2,1,0:T(8,128)(2,1)}, f32[27,32,32]{2,1,0:T(8,128)}, f32[1,32]{1,0:T(1,128)}) custom-call(bf16[8,16,2048]{2,1,0:T(8,128)(2,1)S(1)} %get-tuple-element.8.dx, bf16[2,8,16,128]{3,2,1,0:T(8,128)(2,1)S(1)} %get-tuple-element.9.fin), custom_call_target="tpu_custom_call" | custom-call | tf_op jit(solution)/shard_map/pallas_call | solution.py:519

commit v5 on v3

--- a/solution.py
+++ b/solution.py
@@ -32,7 +32,7 @@
 
 
 def kernel(comm, vol_hbm, cot_hbm, w_hbm, b_hbm, dx, fin, vol, cot, wbuf, bbuf, nv, nc,
-           s, c, gp, t1, t2, tb, dq, part16, rs, xs, zs, ssem, rsem, lsem):
+           s, c, gp, t1, t2, tb, dq, part16, rs, xs, zs, ssem, rsem, lsem, ring):
     loads = [pltpu.make_async_copy(a, b, lsem.at[i]) for i, (a, b) in enumerate(
         ((vol_hbm, vol), (cot_hbm, cot), (w_hbm, wbuf), (b_hbm, bbuf)))]
     for load in loads:
@@ -53,7 +53,9 @@
         gx_peers = [at(gx + k, gy) for k in range(1, 8)]
         x_peers = [at(gx, zi * X_CHIPS + lax.rem(xi + k, X_CHIPS)) for k in range(1, X_CHIPS)]
         z_peers = [at(gx, lax.rem(zi + k, Z_CHIPS) * X_CHIPS + xi) for k in range(1, Z_CHIPS)]
-        peers = z_peers + [at(gx + a, gy + b) for a, b in around if b] + gx_peers + x_peers
+        z_near = [z_peers[0], z_peers[Z_CHIPS - 2]]
+        z_next = [z_peers[1], z_peers[Z_CHIPS - 3]]
+        peers = [at(gx + a, gy + b) for a, b in around if b] + gx_peers + x_peers + z_near
         barrier = pltpu.get_barrier_semaphore()
         for peer in peers:
             pl.semaphore_signal(barrier, inc=1, device_id=peer, device_id_type=MESH)
@@ -93,6 +95,8 @@
     turn(vol, nv, 2, 32)
     if comm:
         pl.semaphore_wait(barrier, len(peers))
+        for peer in z_near:
+            pl.semaphore_signal(ring.at[0], inc=1, device_id=peer, device_id_type=MESH)
         wave1 = [
             send(nv.at[2, 32:288], nv.at[10, 32:288], at(gx - 1, gy)),
             send(nv.at[9, 32:288], nv.at[1, 32:288], at(gx + 1, gy)),
@@ -162,6 +166,9 @@
         preferred_element_type=F32, precision=lax.Precision.HIGHEST)
 
     if comm:
+        pl.semaphore_wait(ring.at[0], 2)
+        for peer in z_next:
+            pl.semaphore_signal(ring.at[1], inc=1, device_id=peer, device_id_type=MESH)
         for copy in wave1:
             copy.wait()
 
@@ -277,6 +284,7 @@
 
     own = range(1, 5)
     right = jnp.concatenate([tiles(gp, 1, own, 32, 288), tiles(gp, 1, own, 288, 544)], axis=1)
+    sums = gathered(lax.dot_general(jnp.ones((16, 1024), BF), right, NT, preferred_element_type=F32), 16, 0)
     blocks = []
     for kx in range(3):
         for kz in range(3):
@@ -288,21 +296,19 @@
             while len(blocks) >= 4:
                 put(blocks[:4])
                 blocks = blocks[4:]
-    wide = lax.dot_general(jnp.ones((16, 1024), BF), right, NT, preferred_element_type=F32)
-    total = gathered(wide, 16, 0)
-    put(blocks + [jnp.concatenate([total, total], axis=0)])
+    put(blocks + [jnp.concatenate([sums, sums], axis=0)])
     part16[7] = jnp.zeros((32, 128), BF)
 
     def later_halo():
+        @pl.loop(1, 5)
+        def _(j):
+            turn_gp(j, 1, 17)
+
         base = sum(jnp.dot(jnp.concatenate([stacked_rows(kk, 2 - d) for kk in range(9)], axis=0),
                            one_hot(32, 128, lambda r, q: (q // 32 == d) & (r == natural(q))).astype(BF),
                            preferred_element_type=F32) for d in range(3)).astype(BF)
         for kk in range(9):
             spread(t2, kk, base[kk * 32:(kk + 1) * 32])
-
-        @pl.loop(1, 5)
-        def _(j):
-            turn_gp(j, 1, 17)
 
         if comm:
             for copy in wave2:
@@ -412,6 +418,7 @@
         backward(1)
         for copy in round2:
             copy.wait()
+        pl.semaphore_wait(ring.at[1], 2)
         zs[zi] = split(summed(xs, X_CHIPS, gx), gx)
         round3 = [send(zs.at[zi], zs.at[zi], z_peers[k]) for k in range(Z_CHIPS - 1)]
         backward(2)
@@ -484,6 +491,7 @@
             pltpu.SemaphoreType.DMA((52,)),
             pltpu.SemaphoreType.DMA((52,)),
             pltpu.SemaphoreType.DMA((4,)),
+            pltpu.SemaphoreType.REGULAR((2,)),
         ],
         compiler_params=pltpu.CompilerParams(
             collective_id=0 if comm else None, has_side_effects=comm, vmem_limit_bytes=48 << 20),

time: 36.9 us -> 36.5 us (0.989)
  Pallas kernels: 36.1 us -> 35.7 us
    pallas_call x1, Pallas kernels: 35 us -> 34.6 us  [shards(): pl.pallas_call(functools.partial(kernel, comm), out_shape=(jax.ShapeDtype...]
where the time goes in v5:
time: 36.5 us; the launch traced here: 36.4 us
  Pallas kernels  35.7 us (98%)
  between operations  0.64 us (2%)
    pallas_call x1, Pallas kernels, shards(): pl.pallas_call(functools.partial(kernel, comm), out_shape=(jax.ShapeDtype...  34.6 us
    pallas_call x1, Pallas kernels, shards(): pl.pallas_call(functools.partial(finish, 1.0 / math.sqrt(cells)), out_sha...  1.09 us

profile of v5, /device:TPU:1, one launch (start us, length us, event | category | flops | bytes accessed | tf_op | source)
XLA Modules:
  0.0 36.4 jit_solution(1135953293576755966)
XLA Ops:
  0.6 34.6 %shard_map.67 = (bf16[8,16,2048]{2,1,0:T(8,128)(2,1)S(1)}, bf16[8,32,128]{2,1,0:T(8,128)(2,1)S(1)}) custom-call(bf16[8,16,2048]{2,1,0:T(8,128)(2,1)} %vol_hbm.1, bf16[8,16,2048]{2,1,0:T(8,128)(2,1)} %cot_hbm.1, bf16[27,32,32]{2,1,0:T(8,128)(2,1)} %bitcast.4, f32[1,32]{1,0:T(1,128)} %bitcast.5), custom_call_target="tpu_custom_call" | custom-call | tf_op jit(solution)/shard_map/pallas_call | solution.py:468
  35.3 1.1 %shard_map.68 = (bf16[8,16,2048]{2,1,0:T(8,128)(2,1)}, f32[27,32,32]{2,1,0:T(8,128)}, f32[1,32]{1,0:T(1,128)}) custom-call(bf16[8,16,2048]{2,1,0:T(8,128)(2,1)S(1)} %get-tuple-element.8.dx, bf16[8,32,128]{2,1,0:T(8,128)(2,1)S(1)} %get-tuple-element.9.fin), custom_call_target="tpu_custom_call" | custom-call | tf_op jit(solution)/shard_map/pallas_call | solution.py:499

commit v6 on v5

--- a/solution.py
+++ b/solution.py
@@ -238,7 +238,10 @@
             pre = acc[:, e * 128:(e + 1) * 128] + tb[r0:r1]
             sig = 0.5 * jnp.tanh(0.5 * pre) + 0.5
             grad = c[cell, y:y + r1 - r0].astype(F32)
-            gp[1, cell, y:y + r1 - r0] = (grad * sig * (1.0 + pre * (1.0 - sig))).astype(BF)
+            block = (grad * sig * (1.0 + pre * (1.0 - sig))).astype(BF)
+            gp[1, cell, y:y + r1 - r0] = block
+            gp[0, cell, y:y + r1 - r0] = shifted(block, 127, z_last)
+            gp[2, cell, y:y + r1 - r0] = shifted(block, 1, z_first)
 
     def forward(r0, r1, y_in, y_out, cells):
         rhs = jnp.concatenate(
@@ -247,21 +250,15 @@
         acc = jnp.dot(filter_rows(t1, r0, r1), rhs, preferred_element_type=F32)
         activate(acc, r0, r1, cells, y_out * 32)
 
-    for n in range(2):
-        cells = (2 * n + 1, 2 * n + 2)
-        forward(0, 192, 1, 1, cells)
-        forward(0, 192, 7, 7, cells)
-        forward(64, 192, 11, 13, cells)
+    for b in range(8):
+        for cells in ((1, 2), (3, 4)):
+            rhs = jnp.concatenate(
+                [tiles(s, kz, [cell + kx for cell in cells], (2 * b + 1) * 32, (2 * b + 5) * 32)
+                 for kx in range(3) for kz in range(3)], axis=0)
+            acc = jnp.dot(filter_rows(t1, 0, 64, (0,)), rhs, preferred_element_type=F32)
+            activate(acc, 0, 64, cells, (2 * b + 1) * 32)
 
     group = lane // 32
-
-    def gathered(wide, rows, step):
-        cells = [wide[step * q:step * q + rows, :128] + wide[step * (q + 4):step * (q + 4) + rows, 128:]
-                 for q in range(4)]
-        total = jnp.where(group == 0, cells[0], jnp.where(group == 1, cells[1],
-                          jnp.where(group == 2, cells[2], cells[3])))
-        total = total + pltpu.roll(total, 64, axis=1)
-        return total + pltpu.roll(total, 32, axis=1)
 
     lower = lax.broadcasted_iota(jnp.int32, (32, 128), 0) >= 16
 
@@ -283,33 +280,38 @@
         done.append(0)
 
     own = range(1, 5)
-    right = jnp.concatenate([tiles(gp, 1, own, 32, 288), tiles(gp, 1, own, 288, 544)], axis=1)
-    sums = gathered(lax.dot_general(jnp.ones((16, 1024), BF), right, NT, preferred_element_type=F32), 16, 0)
+    right = jnp.concatenate(
+        [jnp.concatenate([tiles(gp, kz, own, (2 * b + 1) * 32, (2 * b + 3) * 32) for kz in range(3)], axis=0)
+         for b in range(8)], axis=1)
+    even = group % 2 == 0
     blocks = []
+
+    def placed(value, source):
+        turns = (len(done) * 4 + len(blocks) - source) % 4
+        blocks.append(pltpu.roll(value, 32 * turns, axis=1) if turns else value)
+        if len(blocks) == 4:
+            put(blocks)
+            blocks.clear()
+
     for kx in range(3):
+        left = jnp.concatenate(
+            [tiles(s, 1, [kx + cell for cell in own], (2 * b + 1) * 32, (2 * b + 5) * 32)
+             for b in range(8)], axis=1)
+        if kx == 0:
+            left = jnp.concatenate([left, jnp.ones((16, 4096), BF)], axis=0)
+        wide = lax.dot_general(left, right, NT, preferred_element_type=F32)
+        wide = [wide[:, :128], jnp.concatenate([wide[:, 128:], jnp.zeros_like(wide[:, 128:])], axis=1)]
+        if kx == 0:
+            sums = wide[0][128:144] + pltpu.roll(wide[0][128:144], 96, axis=1)
         for kz in range(3):
-            cells = [kx + cell for cell in own]
-            left = jnp.concatenate([tiles(s, kz, cells, 32, 352), tiles(s, kz, cells, 288, 608)], axis=1)
-            wide = lax.dot_general(left, right, NT, preferred_element_type=F32)
-            total = gathered(wide, 96, 32)
-            blocks += [total[ky * 32:(ky + 1) * 32] for ky in range(3)]
-            while len(blocks) >= 4:
-                put(blocks[:4])
-                blocks = blocks[4:]
-    put(blocks + [jnp.concatenate([sums, sums], axis=0)])
+            for ky in range(3):
+                half = wide[kz // 2]
+                both = jnp.where(even, half[ky * 32:ky * 32 + 32], half[ky * 32 + 32:ky * 32 + 64])
+                placed(both + pltpu.roll(both, 96, axis=1), 2 * (kz % 2))
+    placed(jnp.concatenate([sums, sums], axis=0), 2)
     part16[7] = jnp.zeros((32, 128), BF)
 
     def later_halo():
-        @pl.loop(1, 5)
-        def _(j):
-            turn_gp(j, 1, 17)
-
-        base = sum(jnp.dot(jnp.concatenate([stacked_rows(kk, 2 - d) for kk in range(9)], axis=0),
-                           one_hot(32, 128, lambda r, q: (q // 32 == d) & (r == natural(q))).astype(BF),
-                           preferred_element_type=F32) for d in range(3)).astype(BF)
-        for kk in range(9):
-            spread(t2, kk, base[kk * 32:(kk + 1) * 32])
-
         if comm:
             for copy in wave2:
                 copy.wait()
@@ -342,6 +344,11 @@
                 wipe(nv.at[11, 288:304], 16, 128)
                 wipe(nc.at[:, 272:288], 10, 16, 128)
 
+        base = sum(jnp.dot(jnp.concatenate([stacked_rows(kk, 2 - d) for kk in range(9)], axis=0),
+                           one_hot(32, 128, lambda r, q: (q // 32 == d) & (r == natural(q))).astype(BF),
+                           preferred_element_type=F32) for d in range(3)).astype(BF)
+        for kk in range(9):
+            spread(t2, kk, base[kk * 32:(kk + 1) * 32])
         for j in (0, 7):
             fill_s(j, 0, 20)
         for j in range(1, 7):
@@ -361,19 +368,9 @@
                      for kx in range(3) for kz in range(3)], axis=0)
                 acc = jnp.dot(filter_rows(t1, r0, r0 + 32, (half,)), rhs, preferred_element_type=F32)
                 activate(acc, r0, r0 + 32, cells, y_out * 32)
-        for j in (0, 5):
-            turn_gp(j, 0, 18)
-        for j in own:
-            turn_gp(j, 0, 1)
-            turn_gp(j, 17, 18)
 
     def stacked_rows(kk, ky):
         return stacked[kk][ky * 32:(ky + 1) * 32]
-
-    def turn_gp(j, y0, y1):
-        block = gp[1, j, y0 * 32:y1 * 32]
-        gp[0, j, y0 * 32:y1 * 32] = shifted(block, 127, z_last)
-        gp[2, j, y0 * 32:y1 * 32] = shifted(block, 1, z_first)
 
     def backward(b):
         start, r0 = ((0, 0), (6, 0), (10, 64))[b]

time: 36.5 us -> 36.6 us (level)
  no operation moved by 1% of the time
where the time goes in v6:
time: 36.6 us; the launch traced here: 36.4 us
  Pallas kernels  35.8 us (98%)
  between operations  0.64 us (2%)
    pallas_call x1, Pallas kernels, shards(): pl.pallas_call(functools.partial(kernel, comm), out_shape=(jax.ShapeDtype...  34.7 us
    pallas_call x1, Pallas kernels, shards(): pl.pallas_call(functools.partial(finish, 1.0 / math.sqrt(cells)), out_sha...  1.09 us

profile of v6, /device:TPU:1, one launch (start us, length us, event | category | flops | bytes accessed | tf_op | source)
XLA Modules:
  0.0 36.4 jit_solution(5626335077262822313)
XLA Ops:
  0.6 34.7 %shard_map.67 = (bf16[8,16,2048]{2,1,0:T(8,128)(2,1)S(1)}, bf16[8,32,128]{2,1,0:T(8,128)(2,1)S(1)}) custom-call(bf16[8,16,2048]{2,1,0:T(8,128)(2,1)} %vol_hbm.1, bf16[8,16,2048]{2,1,0:T(8,128)(2,1)} %cot_hbm.1, bf16[27,32,32]{2,1,0:T(8,128)(2,1)} %bitcast.4, f32[1,32]{1,0:T(1,128)} %bitcast.5), custom_call_target="tpu_custom_call" | custom-call | tf_op jit(solution)/shard_map/pallas_call | solution.py:465
  35.4 1.1 %shard_map.68 = (bf16[8,16,2048]{2,1,0:T(8,128)(2,1)}, f32[27,32,32]{2,1,0:T(8,128)}, f32[1,32]{1,0:T(1,128)}) custom-call(bf16[8,16,2048]{2,1,0:T(8,128)(2,1)S(1)} %get-tuple-element.8.dx, bf16[8,32,128]{2,1,0:T(8,128)(2,1)S(1)} %get-tuple-element.9.fin), custom_call_target="tpu_custom_call" | custom-call | tf_op jit(solution)/shard_map/pallas_call | solution.py:496

commit v7 on v6

--- a/solution.py
+++ b/solution.py
@@ -111,67 +111,7 @@
                                   nv.at[inner_x[a][1], inner_y[b][1]], at(gx + a, gy + b)))
     loads[1].wait()
     turn(cot, nc, 1, 16)
-
-    def paired(buf, j, r0, r1):
-        rows = (r1 - r0) // 16
-        a = buf[j, r0:r1]
-        b = buf[j + 4, r0:r1]
-        even = jnp.where(low, a, pltpu.roll(b, 64, axis=1))
-        odd = jnp.where(low, pltpu.roll(a, 64, axis=1), b)
-        both = jnp.concatenate(
-            [even.reshape(rows, 1, 16, 128), odd.reshape(rows, 1, 16, 128)], axis=1)
-        return both.reshape(rows * 32, 128)
-
-    def fill_s(j, y0, y1):
-        block = paired(nv, j, y0 * 16, y1 * 16)
-        s[1, j, y0 * 32:y1 * 32] = block
-        s[0, j, y0 * 32:y1 * 32] = shifted(block, 1, z_first)
-        s[2, j, y0 * 32:y1 * 32] = shifted(block, 127, z_last)
-
-    def fill_c(j, y0, y1):
-        c[j, y0 * 32:y1 * 32] = paired(nc, j, y0 * 16, y1 * 16)
-
-    @pl.loop(2, 6)
-    def _(j):
-        fill_s(j, 2, 18)
-
-    @pl.loop(1, 5)
-    def _(j):
-        fill_c(j, 1, 17)
-
-    def spread(t, kk, base):
-        turned = [base] + [pltpu.roll(base, 32 * i, axis=1) for i in (1, 2, 3)]
-        zero = jnp.zeros_like(base)
-        rows = [(base, zero), (turned[1], zero),
-                (jnp.where(lane >= 64, turned[2], zero), jnp.where(lane < 64, turned[2], zero)),
-                (jnp.where(lane >= 96, turned[3], zero), jnp.where(lane < 96, turned[3], zero)),
-                (zero, base), (zero, turned[1])]
-        for yo in range(6):
-            for half in range(2):
-                t[2 * kk + half, yo * 32:(yo + 1) * 32] = rows[yo][half]
-
-    loads[2].wait()
-    loads[3].wait()
-    rows4 = one_hot(128, 128, lambda r, q: (r // 32 == q // 32) & (q % 32 == natural(r))).astype(BF)
-    lanes1 = one_hot(32, 32, lambda r, q: q == natural(r)).astype(BF)
-    stacked = []
-    for kk in range(9):
-        raw = jnp.concatenate([wbuf[(kk // 3) * 9 + ky * 3 + kk % 3] for ky in range(3)]
-                              + [jnp.zeros((32, 32), BF)], axis=0)
-        stacked.append(jnp.dot(rows4, raw, preferred_element_type=F32).astype(BF))
-        spread(t1, kk, lax.dot_general(lanes1, stacked[kk], NT, preferred_element_type=F32).astype(BF))
-    tb[...] = lax.dot_general(
-        one_hot(192, 32, lambda r, q: q == natural(r)),
-        jnp.broadcast_to(bbuf[...], (128, 32)), NT,
-        preferred_element_type=F32, precision=lax.Precision.HIGHEST)
-
     if comm:
-        pl.semaphore_wait(ring.at[0], 2)
-        for peer in z_next:
-            pl.semaphore_signal(ring.at[1], inc=1, device_id=peer, device_id_type=MESH)
-        for copy in wave1:
-            copy.wait()
-
         wave2 = [
             send(nv.at[3, 32:288], nv.at[11, 32:288], at(gx - 1, gy)),
             send(nv.at[8, 32:288], nv.at[0, 32:288], at(gx + 1, gy)),
@@ -196,6 +136,71 @@
             wave2.append(send(nc.at[side_x[a][0], side_y[b][0]],
                               nc.at[side_x[a][1], side_y[b][1]], at(gx + a, gy + b)))
 
+    def paired(buf, j, r0, r1):
+        rows = (r1 - r0) // 16
+        a = buf[j, r0:r1]
+        b = buf[j + 4, r0:r1]
+        even = jnp.where(low, a, pltpu.roll(b, 64, axis=1))
+        odd = jnp.where(low, pltpu.roll(a, 64, axis=1), b)
+        both = jnp.concatenate(
+            [even.reshape(rows, 1, 16, 128), odd.reshape(rows, 1, 16, 128)], axis=1)
+        return both.reshape(rows * 32, 128)
+
+    def fill_s(j, y0, y1):
+        block = paired(nv, j, y0 * 16, y1 * 16)
+        s[1, j, y0 * 32:y1 * 32] = block
+        s[0, j, y0 * 32:y1 * 32] = shifted(block, 1, z_first)
+        s[2, j, y0 * 32:y1 * 32] = shifted(block, 127, z_last)
+
+    def fill_c(j, y0, y1):
+        c[j, y0 * 32:y1 * 32] = paired(nc, j, y0 * 16, y1 * 16)
+
+    @pl.loop(2, 6)
+    def _(j):
+        fill_s(j, 2, 18)
+
+    @pl.loop(1, 5)
+    def _(j):
+        fill_c(j, 1, 17)
+
+    def spread(t, kk, base):
+        turned = [base] + [pltpu.roll(base, 32 * i, axis=1) for i in (1, 2, 3)]
+        zero = jnp.zeros_like(base)
+        rows = [(base, zero), (turned[1], zero),
+                (jnp.where(lane >= 64, turned[2], zero), jnp.where(lane < 64, turned[2], zero)),
+                (jnp.where(lane >= 96, turned[3], zero), jnp.where(lane < 96, turned[3], zero)),
+                (zero, base), (zero, turned[1])]
+        for yo in range(6):
+            for half in range(2):
+                t[2 * kk + half, yo * 32:(yo + 1) * 32] = rows[yo][half]
+
+    loads[2].wait()
+    loads[3].wait()
+    rows4 = one_hot(128, 128, lambda r, q: (r // 32 == q // 32) & (q % 32 == natural(r))).astype(BF)
+    lanes1 = one_hot(32, 32, lambda r, q: q == natural(r)).astype(BF)
+    stacked = []
+    for kk in range(9):
+        raw = jnp.concatenate([wbuf[(kk // 3) * 9 + ky * 3 + kk % 3] for ky in range(3)]
+                              + [jnp.zeros((32, 32), BF)], axis=0)
+        stacked.append(jnp.dot(rows4, raw, preferred_element_type=F32).astype(BF))
+        spread(t1, kk, lax.dot_general(lanes1, stacked[kk], NT, preferred_element_type=F32).astype(BF))
+    base = sum(jnp.dot(jnp.concatenate([stacked[kk][(2 - d) * 32:(3 - d) * 32] for kk in range(9)], axis=0),
+                       one_hot(32, 128, lambda r, q: (q // 32 == d) & (r == natural(q))).astype(BF),
+                       preferred_element_type=F32) for d in range(3)).astype(BF)
+    for kk in range(9):
+        spread(t2, kk, base[kk * 32:(kk + 1) * 32])
+    tb[...] = lax.dot_general(
+        one_hot(192, 32, lambda r, q: q == natural(r)),
+        jnp.broadcast_to(bbuf[...], (128, 32)), NT,
+        preferred_element_type=F32, precision=lax.Precision.HIGHEST)
+
+    if comm:
+        pl.semaphore_wait(ring.at[0], 2)
+        for peer in z_next:
+            pl.semaphore_signal(ring.at[1], inc=1, device_id=peer, device_id_type=MESH)
+        for copy in wave1:
+            copy.wait()
+
         @pl.when(gx == 0)
         def _():
             wipe(nv.at[1, 16:304], 288, 128)
@@ -344,11 +349,6 @@
                 wipe(nv.at[11, 288:304], 16, 128)
                 wipe(nc.at[:, 272:288], 10, 16, 128)
 
-        base = sum(jnp.dot(jnp.concatenate([stacked_rows(kk, 2 - d) for kk in range(9)], axis=0),
-                           one_hot(32, 128, lambda r, q: (q // 32 == d) & (r == natural(q))).astype(BF),
-                           preferred_element_type=F32) for d in range(3)).astype(BF)
-        for kk in range(9):
-            spread(t2, kk, base[kk * 32:(kk + 1) * 32])
         for j in (0, 7):
             fill_s(j, 0, 20)
         for j in range(1, 7):
@@ -368,9 +368,6 @@
                      for kx in range(3) for kz in range(3)], axis=0)
                 acc = jnp.dot(filter_rows(t1, r0, r0 + 32, (half,)), rhs, preferred_element_type=F32)
                 activate(acc, r0, r0 + 32, cells, y_out * 32)
-
-    def stacked_rows(kk, ky):
-        return stacked[kk][ky * 32:(ky + 1) * 32]
 
     def backward(b):
         start, r0 = ((0, 0), (6, 0), (10, 64))[b]
@@ -441,6 +438,7 @@
     out.start()
     swap = one_hot(128, 128, lambda r, q: r == (q // 32) * 32 + (q % 2) * 16 + (q % 32) // 2).astype(BF)
     final = jnp.dot(fin[...].reshape(256, 128), swap, preferred_element_type=F32) * scale
+    others = []
     for t in range(27):
         block = final[(t // 4) * 32:(t // 4) * 32 + 32]
         if t % 4:
@@ -448,10 +446,13 @@
         k = (t // 9) * 9 + (t % 3) * 3 + (t // 3) % 3
         df[k, pl.ds(0, 16, stride=2), :] = block[0:16, 0:32]
         df[k, pl.ds(1, 16, stride=2), :] = block[16:32, 0:32]
+        if t % 9 == 8:
+            planes = slice(t - 8, t + 1)
+            others.append(pltpu.make_async_copy(df.at[planes], df_hbm.at[planes], sem.at[1 + t // 9]))
+            others[-1].start()
     db[...] = pltpu.roll(final[192:200] + final[208:216], 32, axis=1)[0:1, 0:32]
-    others = [pltpu.make_async_copy(df, df_hbm, sem.at[1]), pltpu.make_async_copy(db, db_hbm, sem.at[2])]
-    for copy in others:
-        copy.start()
+    others.append(pltpu.make_async_copy(db, db_hbm, sem.at[4]))
+    others[-1].start()
     for copy in [out] + others:
         copy.wait()
 
@@ -501,7 +502,7 @@
         in_specs=[vm, vm],
         out_specs=[pl.BlockSpec(memory_space=pl.ANY)] * 3,
         scratch_shapes=[pltpu.VMEM((27, C, C), F32), pltpu.VMEM((1, C), F32),
-                        pltpu.SemaphoreType.DMA((3,))],
+                        pltpu.SemaphoreType.DMA((5,))],
         compiler_params=pltpu.CompilerParams(vmem_limit_bytes=4 << 20),
     )(dx, fin)
     return dg, df.reshape(3, 3, 3, C, C), db.reshape(C)

time: 36.6 us -> 36.6 us (level)
  no operation moved by 1% of the time
where the time goes in v7:
time: 36.6 us; the launch traced here: 36.5 us
  Pallas kernels  35.8 us (98%)
  between operations  0.64 us (2%)
    pallas_call x1, Pallas kernels, shards(): pl.pallas_call(functools.partial(kernel, comm), out_shape=(jax.ShapeDtype...  34.8 us
    pallas_call x1, Pallas kernels, shards(): pl.pallas_call(functools.partial(finish, 1.0 / math.sqrt(cells)), out_sha...  1.06 us

profile of v7, /device:TPU:1, one launch (start us, length us, event | category | flops | bytes accessed | tf_op | source)
XLA Modules:
  0.0 36.5 jit_solution(16312588773297111180)
XLA Ops:
  0.6 34.8 %shard_map.67 = (bf16[8,16,2048]{2,1,0:T(8,128)(2,1)S(1)}, bf16[8,32,128]{2,1,0:T(8,128)(2,1)S(1)}) custom-call(bf16[8,16,2048]{2,1,0:T(8,128)(2,1)} %vol_hbm.1, bf16[8,16,2048]{2,1,0:T(8,128)(2,1)} %cot_hbm.1, bf16[27,32,32]{2,1,0:T(8,128)(2,1)} %bitcast.4, f32[1,32]{1,0:T(1,128)} %bitcast.5), custom_call_target="tpu_custom_call" | custom-call | tf_op jit(solution)/shard_map/pallas_call | solution.py:466
  35.4 1.1 %shard_map.68 = (bf16[8,16,2048]{2,1,0:T(8,128)(2,1)}, f32[27,32,32]{2,1,0:T(8,128)}, f32[1,32]{1,0:T(1,128)}) custom-call(bf16[8,16,2048]{2,1,0:T(8,128)(2,1)S(1)} %get-tuple-element.8.dx, bf16[8,32,128]{2,1,0:T(8,128)(2,1)S(1)} %get-tuple-element.9.fin), custom_call_target="tpu_custom_call" | custom-call | tf_op jit(solution)/shard_map/pallas_call | solution.py:497

commit v8 on v7

--- a/solution.py
+++ b/solution.py
@@ -403,18 +403,18 @@
     if comm:
         round1 = [send(part16.at[lax.rem(gx + k + 1, 8)], rs.at[k], gx_peers[k]) for k in range(7)]
         rs[7] = part16[gx]
-        later_halo()
         for copy in round1:
             copy.wait()
         xs[xi] = split(summed(rs, 8, gx), gx)
         round2 = [send(xs.at[xi], xs.at[xi], x_peers[k]) for k in range(X_CHIPS - 1)]
-        backward(0)
-        backward(1)
+        later_halo()
         for copy in round2:
             copy.wait()
         pl.semaphore_wait(ring.at[1], 2)
         zs[zi] = split(summed(xs, X_CHIPS, gx), gx)
         round3 = [send(zs.at[zi], zs.at[zi], z_peers[k]) for k in range(Z_CHIPS - 1)]
+        backward(0)
+        backward(1)
         backward(2)
         emit()
         for copy in round3:

time: 36.6 us -> 36.7 us (level)
  no operation moved by 1% of the time
where the time goes in v8:
time: 36.7 us; the launch traced here: 36.6 us
  Pallas kernels  35.9 us (98%)
  between operations  0.64 us (2%)
    pallas_call x1, Pallas kernels, shards(): pl.pallas_call(functools.partial(kernel, comm), out_shape=(jax.ShapeDtype...  34.9 us
    pallas_call x1, Pallas kernels, shards(): pl.pallas_call(functools.partial(finish, 1.0 / math.sqrt(cells)), out_sha...  1.06 us

profile of v8, /device:TPU:1, one launch (start us, length us, event | category | flops | bytes accessed | tf_op | source)
XLA Modules:
  0.0 36.6 jit_solution(10084157054966734395)
XLA Ops:
  0.6 34.9 %shard_map.67 = (bf16[8,16,2048]{2,1,0:T(8,128)(2,1)S(1)}, bf16[8,32,128]{2,1,0:T(8,128)(2,1)S(1)}) custom-call(bf16[8,16,2048]{2,1,0:T(8,128)(2,1)} %vol_hbm.1, bf16[8,16,2048]{2,1,0:T(8,128)(2,1)} %cot_hbm.1, bf16[27,32,32]{2,1,0:T(8,128)(2,1)} %bitcast.4, f32[1,32]{1,0:T(1,128)} %bitcast.5), custom_call_target="tpu_custom_call" | custom-call | tf_op jit(solution)/shard_map/pallas_call | solution.py:466
  35.5 1.1 %shard_map.68 = (bf16[8,16,2048]{2,1,0:T(8,128)(2,1)}, f32[27,32,32]{2,1,0:T(8,128)}, f32[1,32]{1,0:T(1,128)}) custom-call(bf16[8,16,2048]{2,1,0:T(8,128)(2,1)S(1)} %get-tuple-element.8.dx, bf16[8,32,128]{2,1,0:T(8,128)(2,1)S(1)} %get-tuple-element.9.fin), custom_call_target="tpu_custom_call" | custom-call | tf_op jit(solution)/shard_map/pallas_call | solution.py:497
